TPU v7x, 256 devices: a whole 4x4x8 slice. The times are simulated.
256 devices in a mesh: row: 16 (over z_hi, x), col: 16 (over y, z_lo, core).
Axes of the slice: x: 4, y: 4, z: 8 (z_hi: 4, z_lo: 2; z = z_hi * 2 + z_lo), core: 2. Of those that a mesh axis runs over, the one named last changes fastest.
Arguments:
- panels: int32 [1], replicated, may hold values from 0 to 15
- inverse: float32 [16384, 16384], P('row', 'col'), may hold values from -4 to 28, as said below
- weight: float32 [1024, 16384], P('row', 'col'), may hold values from -0.046875 to 0.046875
- tokens: bfloat16 [2048, 16384], P('row', 'col'), may hold values from -6 to 6
- targets: bfloat16 [2048, 1024], P('row', 'col'), may hold values from -6 to 6
Outputs:
- new_inverse: float32 [16384, 16384], P('row', 'col')
- pruned: float32 [1024, 16384], P('row', 'col')
- residual: float32 [2048, 1024], P('row', 'col')
- correlation: float32 [1024, 16384], P('row', 'col')
Inputs may be any that keep to these rules, and one draw needn't show every extreme that they name: `inverse`: symmetric and positive definite.
All inputs are finite; a program needn't handle non-finite values.
Results may differ from a plain program's by a relative error of at most 0.0035.
Values may be sent and summed in bfloat16 or wider, within the bound.
A program may use at most 128 MiB of HBM per device.

v0:
```python
import math

import jax
import jax.numpy as jnp
from jax import lax
from jax.sharding import PartitionSpec as P

PW = 1024


def broadcast(array, axis, root):
    mine = lax.axis_index(axis) == root
    return lax.psum(jnp.where(mine, array, jnp.zeros_like(array)), axis)


def cholesky_apply(factor, right_side):
    halfway = lax.linalg.triangular_solve(
        factor, right_side, left_side=True, lower=True, transpose_a=False
    )
    return lax.linalg.triangular_solve(
        factor, halfway, left_side=True, lower=True, transpose_a=True
    )


def shards(panels, inverse, weight, tokens, targets):
    highest = lax.Precision.HIGHEST
    rows_local = inverse.shape[0]
    cols_local = inverse.shape[1]
    out_local = targets.shape[1]
    anchor = panels[0] * PW
    owner_col = anchor // cols_local
    owner_row = anchor // rows_local
    holds_panel = lax.axis_index("col") == owner_col
    col_slab = inverse
    weight_slab = weight
    col_slab = jnp.where(holds_panel, col_slab, jnp.zeros_like(col_slab))
    weight_slab = jnp.where(holds_panel, weight_slab, jnp.zeros_like(weight_slab))
    col_share, weight_share = (
        lax.psum_scatter(col_slab, "col", scatter_dimension=0, tiled=True),
        lax.psum_scatter(weight_slab, "col", scatter_dimension=0, tiled=True),
    )
    col_slab, weight_slab = (
        lax.all_gather(col_share, "col", axis=0, tiled=True),
        lax.all_gather(weight_share, "col", axis=0, tiled=True),
    )
    is_owner = lax.axis_index("row") == owner_row
    safe_block = jnp.where(is_owner, col_slab, jnp.eye(PW, dtype=jnp.float32))
    factor = jnp.linalg.cholesky(safe_block)
    solved = cholesky_apply(factor, inverse)
    solved = broadcast(solved, "row", owner_row)
    new_inverse = inverse - jnp.dot(
        col_slab, solved, precision=highest, preferred_element_type=jnp.float32
    )
    pruned = weight - jnp.dot(
        weight_slab, solved, precision=highest, preferred_element_type=jnp.float32
    )
    pruned_low = pruned.astype(jnp.bfloat16)
    partial_value = lax.dot_general(
        tokens,
        lax.all_gather(pruned_low, "row", axis=0, tiled=True),
        (((1,), (1,)), ((), ())),
        preferred_element_type=jnp.float32,
    )
    col_index = lax.axis_index("col")
    placed = lax.dynamic_update_slice_in_dim(
        jnp.zeros_like(partial_value), targets.astype(jnp.float32), col_index * out_local, 1
    )
    partial_value = partial_value - placed
    residual = lax.psum_scatter(partial_value, "col", scatter_dimension=1, tiled=True)
    residual_low = lax.all_gather(residual.astype(jnp.bfloat16), "col", axis=1, tiled=True)
    token_count = tokens.shape[0] * lax.axis_size("row")
    correlation = lax.psum_scatter(
        lax.dot_general(
            residual_low, tokens, (((0,), (0,)), ((), ())), preferred_element_type=jnp.float32
        ),
        "row",
        scatter_dimension=0,
        tiled=True,
    )
    correlation = correlation * (1.0 / math.sqrt(token_count))
    return (new_inverse, pruned, residual, correlation)


def solution(mesh):
    in_specs = (P(), P("row", "col"), P("row", "col"), P("row", "col"), P("row", "col"))
    out_specs = (P("row", "col"), P("row", "col"), P("row", "col"), P("row", "col"))
    return jax.shard_map(shards, mesh=mesh, in_specs=in_specs, out_specs=out_specs, check_vma=False)
```

profile of v0, /device:TPU:8, one launch (start us, length us, event | category | flops | bytes accessed | tf_op | source)
XLA Modules:
  0.0 1023.9 jit_solution(10012692551235183180)
XLA Ops:
  7.9 5.3 copy.35
  16.1 5.3 copy.70
  21.5 68.5 %reduce-scatter.10.cloned.1.call-done = f32[64,1024]{1,0:T(8,128)} async-done(((f32[1024,1024]{1,0:T(8,128)}), f32[64,1024]{1,0:T(8,128)}) %reduce-scatter.10.cloned.1.call-update) | async-done | bytes 262160 | tf_op jit(solution)/shard_map/reduce_scatter | solution.py:39
  91.0 46.4 %all-gather.4.cloned.1.call-done = f32[1024,1024]{1,0:T(8,128)} async-done(((f32[64,1024]{1,0:T(8,128)}), f32[1024,1024]{1,0:T(8,128)}) %all-gather.4.cloned.1.call-update) | async-done | bytes 4194320 | tf_op jit(solution)/shard_map/all_gather | solution.py:43
  137.3 5.3 copy.37
  145.5 5.5 copy.38
  156.2 11.7 %cholesky.222 = f32[128,128]{1,0:T(8,128)S(1)} custom-call(f32[128,128]{1,0:T(8,128)S(1)} %cholesky.577), custom_call_target="Cholesky" | custom-call | tf_op jit(solution)/shard_map/jit(cholesky)/cholesky | solution.py:48
  168.0 9.8 custom-call.64
  180.9 11.7 %cholesky.243 = f32[128,128]{1,0:T(8,128)S(1)} custom-call(f32[128,128]{1,0:T(8,128)S(1)} %cholesky.581), custom_call_target="Cholesky" | custom-call | tf_op jit(solution)/shard_map/jit(cholesky)/cholesky | solution.py:48
  193.3 9.8 custom-call.65
  208.6 11.7 %cholesky.466 = f32[128,128]{1,0:T(8,128)S(1)} custom-call(f32[128,128]{1,0:T(8,128)S(1)} %cholesky.586), custom_call_target="Cholesky" | custom-call | tf_op jit(solution)/shard_map/jit(cholesky)/cholesky | solution.py:48
  221.1 9.8 custom-call.66
  235.7 11.7 %cholesky.485 = f32[128,128]{1,0:T(8,128)S(1)} custom-call(f32[128,128]{1,0:T(8,128)S(1)} %cholesky.591), custom_call_target="Cholesky" | custom-call | tf_op jit(solution)/shard_map/jit(cholesky)/cholesky | solution.py:48
  248.2 9.8 custom-call.67
  262.3 11.9 %cholesky.504 = f32[128,128]{1,0:T(8,128)S(1)} custom-call(f32[128,128]{1,0:T(8,128)S(1)} %cholesky.596), custom_call_target="Cholesky" | custom-call | tf_op jit(solution)/shard_map/jit(cholesky)/cholesky | solution.py:48
  274.9 9.8 custom-call.68
  289.0 11.7 %cholesky.524 = f32[128,128]{1,0:T(8,128)S(1)} custom-call(f32[128,128]{1,0:T(8,128)S(1)} %cholesky.601), custom_call_target="Cholesky" | custom-call | tf_op jit(solution)/shard_map/jit(cholesky)/cholesky | solution.py:48
  301.5 9.8 custom-call.69
  315.3 11.7 %cholesky.544 = f32[128,128]{1,0:T(8,128)S(1)} custom-call(f32[128,128]{1,0:T(8,128)S(1)} %cholesky.606), custom_call_target="Cholesky" | custom-call | tf_op jit(solution)/shard_map/jit(cholesky)/cholesky | solution.py:48
  327.8 9.8 custom-call.70
  340.7 11.7 %cholesky.562 = f32[128,128]{1,0:T(8,128)S(1)} custom-call(f32[128,128]{1,0:T(8,128)S(1)} %convolution_subtract_fusion.18), custom_call_target="Cholesky" | custom-call | tf_op jit(solution)/shard_map/jit(cholesky)/cholesky | solution.py:48
  362.6 4.9 select_select_fusion
  367.5 23.9 %while.1 = (s32[]{:T(128)}, f32[1024,1024]{0,1:T(8,128)}, s32[8,2]{0,1:T(2,128)S(1)}, f32[8,128,128]{2,1,0:T(8,128)S(1)}, s32[]{:T(128)}) while((s32[]{:T(128)}, f32[1024,1024]{0,1:T(8,128)}, s32[8,2]{0,1:T(2,128)S(1)}, f32[8,128,128]{2,1,0:T(8,128)S(1)}, s32[]{:T(128)}) %tuple.55), condition=%wide.while_cond, body=%wide.while_body.sunk | while | flops 2 | bytes 393321 | solution.py:20
  391.4 78.8 %custom-call.71 = f32[8,128,128]{1,2,0:T(8,128)S(1)} custom-call(f32[8,128,128]{2,1,0:T(8,128)S(1)} %get-tuple-element.11), custom_call_target="InvertDiagBlocksLowerTriangular" | custom-call | tf_op jit(solution)/shard_map/triangular_solve | solution.py:20
  549.5 19.0 %all-gather = f32[16,4,1024]{2,1,0:T(4,128)S(1)} all-gather(f32[1,4,1024]{2,1,0:T(4,128)S(1)} %dynamic-slice_bitcast_fusion), channel_id=1, replica_groups=mesh['row'=16,'col'=16] {'col'}, dimensions={0}, use_global_device_ids=true | all-gather | bytes 278528 | tf_op jit(solution)/shard_map/all_gather | solution.py:44
  568.6 202.5 %all-reduce.5.cloned.1.call-done = f32[1024,1024]{0,1:T(8,128)} async-done(((f32[1024,1024]{0,1:T(8,128)}), f32[1024,1024]{0,1:T(8,128)}) %all-reduce.5.cloned.1.call-update) | async-done | bytes 4194320 | tf_op jit(solution)/shard_map/psum | solution.py:13
  771.1 7.0 fusion.112
  778.3 56.1 %all-gather.6.cloned.1.call-done = bf16[1024,1024]{1,0:T(8,128)(2,1)} async-done(((bf16[64,1024]{1,0:T(8,128)(2,1)}), bf16[1024,1024]{1,0:T(8,128)(2,1)}) %all-gather.6.cloned.1.call-update) | async-done | bytes 2097168 | tf_op jit(solution)/shard_map/all_gather | solution.py:60
  837.5 55.6 %reduce-scatter.6.cloned.1.call-done = f32[128,64]{0,1:T(8,128)} async-done(((f32[128,1024]{0,1:T(8,128)}), f32[128,64]{0,1:T(8,128)}) %reduce-scatter.6.cloned.1.call-update) | async-done | bytes 32784 | tf_op jit(solution)/shard_map/reduce_scatter | solution.py:69
  893.8 21.7 %all_gather.15 = bf16[128,1024]{0,1:T(8,128)(2,1)S(1)} all-gather(bf16[128,64]{0,1:T(8,128)(2,1)S(1)} %convert_element_type.15), channel_id=1, replica_groups=mesh['row'=16,'col'=16] {'col'}, dimensions={1}, use_global_device_ids=true | all-gather | bytes 278528 | tf_op jit(solution)/shard_map/all_gather | solution.py:70
  918.3 18.4 %convolution_subtract_fusion = f32[1024,1024]{1,0:T(8,128)} fusion(f32[1024,1024]{1,0:T(8,128)} %param.6, f32[1024,1024]{1,0:T(8,128)} %all-gather.4.cloned.1.call-done, f32[1024,1024]{0,1:T(8,128)} %all-reduce.5.cloned.1.call-done), kind=kOutput, calls=%fused_computation.26 | convolution fusion | flops 12885950464 | bytes 16777216 | tf_op jit(solution)/shard_map/dot_general | solution.py:51
  936.6 78.6 %reduce-scatter.8.cloned.1.call-done = f32[64,1024]{1,0:T(8,128)} async-done(((f32[1024,1024]{1,0:T(8,128)}), f32[64,1024]{1,0:T(8,128)}) %reduce-scatter.8.cloned.1.call-update) | async-done | bytes 262160 | tf_op jit(solution)/shard_map/reduce_scatter | solution.py:72
  (223 shorter events, 160.9 us)
Async XLA Ops:
  7.2 827.2 %copy-start = (bf16[128,1024]{1,0:T(8,128)(2,1)S(1)}, bf16[128,1024]{1,0:T(8,128)(2,1)}, u32[]{:S(2)}) copy-start(bf16[128,1024]{1,0:T(8,128)(2,1)} %param.8) | copy-start | bytes 786436
  7.2 82.9 %reduce-scatter.10.cloned.1.call-start = ((), (), s32[]{:S(2)}) async-start(), calls=%async_computation.8 | async-start | bytes 4456448 | tf_op jit(solution)/shard_map/reduce_scatter | solution.py:39
  21.5 68.7 %copy-start.15 = (f32[64,1024]{1,0:T(8,128)S(1)}, f32[64,1024]{1,0:T(8,128)}, u32[]{:S(2)}) copy-start(f32[64,1024]{1,0:T(8,128)} %param.7) | copy-start | bytes 786436
  21.5 115.8 %all-gather.4.cloned.1.call-start = ((), (), s32[]{:S(2)}) async-start(), calls=%async_computation.3 | async-start | bytes 4456448 | tf_op jit(solution)/shard_map/all_gather | solution.py:43
  90.1 458.6 %all-reduce.7.cloned.1.call-start = ((), (), s32[]{:S(2)}) async-start(), calls=%async_computation.9 | async-start | bytes 524288
  90.9 680.3 %all-reduce.5.cloned.1.call-start = ((), (), s32[]{:S(2)}) async-start(), calls=%async_computation.4 | async-start | bytes 8388608 | tf_op jit(solution)/shard_map/psum | solution.py:13
  154.2 2.0 copy-start.4
  204.2 2.0 copy-start.1
  470.1 23.6 %copy-start.14 = (f32[8,128,128]{1,2,0:T(8,128)}, f32[8,128,128]{1,2,0:T(8,128)S(1)}, u32[]{:S(2)}) copy-start(f32[8,128,128]{1,2,0:T(8,128)S(1)} %custom-call.71) | copy-start | bytes 1572868
  470.1 4.4 copy-start.2
  473.9 3.7 copy-start.3
  474.6 4.8 copy-start.5
  477.5 3.2 copy-start.7
  508.6 4.2 copy-start.6
  526.1 9.0 copy-start.8
  527.8 12.0 %copy-start.13 = (f32[128,1024]{0,1:T(8,128)S(1)}, f32[128,1024]{0,1:T(8,128)}, u32[]{:S(2)}) copy-start(f32[128,1024]{0,1:T(8,128)} %copy.58) | copy-start | bytes 1572868
  527.8 12.9 %copy-start.12 = (f32[128,1024]{0,1:T(8,128)S(1)}, f32[128,1024]{0,1:T(8,128)}, u32[]{:S(2)}) copy-start(f32[128,1024]{0,1:T(8,128)} %copy.59) | copy-start | bytes 1572868
  532.3 9.2 copy-start.11
  532.3 10.0 copy-start.10
  532.3 10.8 %copy-start.9 = (f32[128,1024]{0,1:T(8,128)S(1)}, f32[128,1024]{0,1:T(8,128)}, u32[]{:S(2)}) copy-start(f32[128,1024]{0,1:T(8,128)} %copy.62) | copy-start | bytes 1572868
  546.8 0.7 copy-start.18
  546.8 224.4 %copy-start.16 = (f32[64,1024]{1,0:T(8,128)S(1)}, f32[64,1024]{1,0:T(8,128)}, u32[]{:S(2)}) copy-start(f32[64,1024]{1,0:T(8,128)} %param.7) | copy-start | bytes 786436
  546.8 231.5 %copy-start.17 = (bf16[128,64]{0,1:T(8,128)(2,1)S(1)}, bf16[128,64]{0,1:T(8,128)(2,1)}, u32[]{:S(2)}) copy-start(bf16[128,64]{0,1:T(8,128)(2,1)} %param.9) | copy-start | bytes 49156
  546.8 287.5 %all-gather.6.cloned.1.call-start = ((), (), s32[]{:S(2)}) async-start(), calls=%async_computation.5 | async-start | bytes 2228224 | tf_op jit(solution)/shard_map/all_gather | solution.py:60
  778.2 114.9 %reduce-scatter.6.cloned.1.call-start = ((), (), s32[]{:S(2)}) async-start(), calls=%async_computation.6 | async-start | bytes 557056 | tf_op jit(solution)/shard_map/reduce_scatter | solution.py:69
  837.5 177.7 %reduce-scatter.8.cloned.1.call-start = ((), (), s32[]{:S(2)}) async-start(), calls=%async_computation.7 | async-start | bytes 4456448 | tf_op jit(solution)/shard_map/reduce_scatter | solution.py:72
Sparse Core Ops, SparseCore 0:
  21.6 68.3 reduce-scatter.9
  91.9 45.3 all-gather.3
  140.5 118.2 all-reduce.6
  546.9 224.1 all-reduce.4
  778.3 56.0 all-gather.5
  837.6 55.4 reduce-scatter.5
  918.4 96.8 reduce-scatter.7
where the time goes:
time: 1030 us; the launch traced here: 1020 us
  waiting for transfers between devices  508 us (49%)
  other arithmetic  266 us (26%)
  matrix products  104 us (10%)
  local copies, waits for them, and re-layouts  83.4 us (8%)
  blocking collectives  40.8 us (4%)
  between operations  21.3 us (2%)
    psum x1, waiting for transfers between devices, broadcast(): return lax.psum(jnp.where(mine, array, jnp.zeros_like(array)), axis)  203 us
    another operation x30, other arithmetic, shards(): factor = jnp.linalg.cholesky(safe_block)  167 us
    another operation x3, other arithmetic, cholesky_apply(): lax.linalg.triangular_solve(factor, halfway, left_side=True, lower=True,...  83.7 us
    reduce_scatter x1, waiting for transfers between devices, shards(): lax.psum_scatter(lax.dot_general(residual_low, tokens, (((0,), (0,)), (()...  78.6 us
    reduce_scatter x1, waiting for transfers between devices, shards(): lax.psum_scatter(col_slab, 'col', scatter_dimension=0, tiled=True)  68.5 us
    all_gather x1, waiting for transfers between devices, shards(): lax.all_gather(pruned_low, 'row', axis=0, tiled=True)  56.1 us
    reduce_scatter x1, waiting for transfers between devices, shards(): lax.psum_scatter(partial_value, 'col', scatter_dimension=1, tiled=True)  55.6 us
    all_gather x1, waiting for transfers between devices, shards(): lax.all_gather(col_share, 'col', axis=0, tiled=True)  46.4 us
  transfers between devices with their start and end apart: 7, of which 6 were waited for; matrix products, arithmetic and copies ran while one was open for 41% of the time, Pallas kernels for 0%

commit v1 on v0

v1 whole, which is shorter than its diff:
```python
import functools
import math

import jax
import jax.numpy as jnp
from jax import lax
from jax.experimental import pallas as pl
from jax.experimental.pallas import tpu as pltpu
from jax.sharding import PartitionSpec as P

PW = 1024
NB = 128
MESH = pl.DeviceIdType.MESH
VMEM = pl.BlockSpec(memory_space=pltpu.VMEM)
f32 = jnp.float32
bf16 = jnp.bfloat16


def place():
    i, j = lax.axis_index("row"), lax.axis_index("col")
    return i, j, i // 4, i % 4, j // 4, (j // 2) % 2, j % 2


def row_of(zh, x):
    return (zh % 4) * 4 + x % 4


def col_of(y, zl, c):
    return ((y % 4) * 2 + zl % 2) * 2 + c % 2


class Copies:
    def __init__(self, send, recv):
        self.send, self.recv, self.made = send, recv, []

    def __call__(self, src, dst, device):
        n = len(self.made)
        copy = pltpu.make_async_remote_copy(
            src_ref=src,
            dst_ref=dst,
            send_sem=self.send.at[n],
            recv_sem=self.recv.at[n],
            device_id=device,
            device_id_type=MESH,
        )
        copy.start()
        self.made.append(copy)
        return copy

    def drain(self):
        for copy in self.made:
            copy.wait_send()


def meet(devices):
    barrier = pltpu.get_barrier_semaphore()
    for device in devices:
        pl.semaphore_signal(barrier, inc=1, device_id=device, device_id_type=MESH)
    pl.semaphore_wait(barrier, len(devices))


PR, PC = 32, 1152


def block_kernel(p_ref, h_ref, out_ref, pack, chunk, got, mine, zgot, local, send1, recv1, send, recv):
    i, j, zh, x, y, zl, c = place()
    p = p_ref[0]
    xs = [(row_of(zh, x + d), j) for d in (1, 2, 3)]
    zs = [(row_of(zh + d, x), j) for d in (1, 2, 3)]
    meet([(i, (j + d) % 16) for d in range(1, 16)] + xs + zs)

    scatter = [
        pltpu.make_async_remote_copy(
            src_ref=pack.at[pl.ds(pl.multiple_of(((j + d) % 16) * PR, PR), PR)],
            dst_ref=chunk,
            send_sem=send1.at[d - 1],
            recv_sem=recv1,
            device_id=(i, (j + d) % 16),
            device_id_type=MESH,
        )
        for d in range(1, 16)
    ]

    @pl.when(i == j)
    def _():
        loads = []
        for g in range(4):
            rows = pl.ds(128 * g, 128)
            a, b = 128 * (g + 1), 128 * (8 - g)
            loads.append(pltpu.make_async_copy(h_ref.at[rows, pl.ds(0, a)], pack.at[rows, pl.ds(0, a)], local.at[2 * g]))
            far = pl.ds(128 * (7 - g), 128)
            loads.append(pltpu.make_async_copy(h_ref.at[far, pl.ds(0, b)], pack.at[rows, pl.ds(a, b)], local.at[2 * g + 1]))
        for load in loads:
            load.start()
        for load in loads:
            load.wait()
        for copy in scatter:
            copy.start()
        own = pltpu.make_async_copy(pack.at[pl.ds(pl.multiple_of(j * PR, PR), PR)], chunk, local.at[8])
        own.start()
        own.wait()

    @pl.when(i != j)
    def _():
        scatter[0].wait_recv()

    copies = Copies(send, recv)

    def piece(k):
        return pl.ds(pl.multiple_of((k % 4) * 8, 8), 8)

    firsts = [copies(chunk.at[piece(x + d)], got.at[d - 1], xs[d - 1]) for d in (1, 2, 3)]
    held = jnp.where(i == p, chunk[piece(x), :], 0.0)
    for d in (1, 2, 3):
        firsts[d - 1].wait_recv()
        held = held + jnp.where(row_of(zh, x - d + 4) == p, got[d - 1], 0.0)
    mine[...] = held
    seconds = [copies(mine, zgot.at[d - 1], zs[d - 1]) for d in (1, 2, 3)]
    for d in (1, 2, 3):
        seconds[d - 1].wait_recv()
        held = held + zgot[d - 1]
    out_ref[j, piece(x), :] = held
    thirds = [copies(out_ref.at[j, piece(x)], out_ref.at[j, piece(x)], xs[d - 1]) for d in (1, 2, 3)]
    for copy in thirds:
        copy.wait_recv()

    gather_cols(copies, out_ref, out_ref, PR)
    copies.drain()

    @pl.when(i == j)
    def _():
        for copy in scatter:
            copy.wait_send()


def gather_cols(copies, first, out, rows):
    i, j, zh, x, y, zl, c = place()
    h = rows // 2
    ups, downs, cores = [], [], []
    across = copies(first.at[j], out.at[j], (i, col_of(y, zl + 1, c)))
    up, down = (i, col_of(y + 1, zl, c)), (i, col_of(y + 3, zl, c))
    peer = (i, col_of(y, zl, c + 1))
    for t in (0, 1):
        src = first if t == 0 else out
        if t == 1:
            across.wait_recv()
        s = col_of(y, zl + t, c)
        ups.append(copies(src.at[s], out.at[s], up))
        downs.append(copies(src.at[s], out.at[s], down))
        cores.append(copies(src.at[s], out.at[s], peer))
    halves = []
    for t in (0, 1):
        ups[t].wait_recv()
        s = col_of(y + 3, zl + t, c)
        halves.append(copies(out.at[s, pl.ds(0, h)], out.at[s, pl.ds(0, h)], up))
        cores.append(copies(out.at[s], out.at[s], peer))
        downs[t].wait_recv()
        s = col_of(y + 1, zl + t, c)
        halves.append(copies(out.at[s, pl.ds(h, h)], out.at[s, pl.ds(h, h)], down))
        cores.append(copies(out.at[s], out.at[s], peer))
    for t in (0, 1):
        halves[2 * t].wait_recv()
        halves[2 * t + 1].wait_recv()
        s = col_of(y + 2, zl + t, c)
        cores.append(copies(out.at[s], out.at[s], peer))
    for copy in cores:
        copy.wait_recv()


def block_everywhere(panels, inverse):
    sems = 9 + 25
    return pl.pallas_call(
        block_kernel,
        out_shape=jax.ShapeDtypeStruct((16, PR, PC), f32),
        in_specs=[pl.BlockSpec(memory_space=pltpu.SMEM), pl.BlockSpec(memory_space=pl.ANY)],
        out_specs=VMEM,
        scratch_shapes=[
            pltpu.VMEM((16 * PR, PC), f32),
            pltpu.VMEM((PR, PC), f32),
            pltpu.VMEM((3, 8, PC), f32),
            pltpu.VMEM((8, PC), f32),
            pltpu.VMEM((3, 8, PC), f32),
            pltpu.SemaphoreType.DMA((9,)),
            pltpu.SemaphoreType.DMA((15,)),
            pltpu.SemaphoreType.DMA,
            pltpu.SemaphoreType.DMA((sems,)),
            pltpu.SemaphoreType.DMA((sems,)),
        ],
        compiler_params=pltpu.CompilerParams(collective_id=0, has_side_effects=True, vmem_limit_bytes=24 << 20),
        cost_estimate=pl.CostEstimate(flops=10**9, bytes_accessed=160 * 10**6, transcendentals=0),
        name="block_everywhere",
    )(panels, inverse)


def split(x):
    hi = x.astype(bf16)
    return hi, (x - hi.astype(f32)).astype(bf16)


def dot(a, b):
    return jnp.dot(a, b, preferred_element_type=f32)


def dot3(a, b):
    ah, al = split(a)
    bh, bl = split(b)
    return dot(ah, bh) + (dot(ah, bl) + dot(al, bh))


def pivot_inverse(rows):
    lane = lax.broadcasted_iota(jnp.int32, (8, NB), 1)
    sub = lax.broadcasted_iota(jnp.int32, (8, NB), 0)
    lane1 = lax.broadcasted_iota(jnp.int32, (1, NB), 1)
    rows = list(rows)
    for k in range(0, NB, 2):
        v, s = k // 8, k % 8
        c0 = [jnp.broadcast_to(r[:, k : k + 1], (8, NB)) for r in rows]
        c1 = [jnp.broadcast_to(r[:, k + 1 : k + 2], (8, NB)) for r in rows]
        r0, r1 = rows[v][s : s + 1, :], rows[v][s + 1 : s + 2, :]
        p00, p01 = c0[v][s : s + 1, :], c1[v][s : s + 1, :]
        p10, p11 = c0[v][s + 1 : s + 2, :], c1[v][s + 1 : s + 2, :]
        scale = 1.0 / (p00 * p11 - p01 * p10)
        e0, e1 = lane1 == k, lane1 == k + 1
        r0 = jnp.where(e0, 1.0, jnp.where(e1, 0.0, r0))
        r1 = jnp.where(e1, 1.0, jnp.where(e0, 0.0, r1))
        u0 = jnp.broadcast_to((p11 * scale) * r0 - (p01 * scale) * r1, (8, NB))
        u1 = jnp.broadcast_to((p00 * scale) * r1 - (p10 * scale) * r0, (8, NB))
        cols = (lane == k) | (lane == k + 1)
        for w in range(NB // 8):
            base = jnp.where(cols, 0.0, rows[w]) - c0[w] * u0 - c1[w] * u1
            if w == v:
                base = jnp.where(sub == s, u0, jnp.where(sub == s + 1, u1, base))
            rows[w] = base
    return rows


def inverse_kernel(b_ref, a, piv):
    n = PW
    for g in range(4):
        for r, start in ((g, 0), (7 - g, 128 * (g + 1))):
            for q in range(r + 1):
                lanes = pl.ds(start + 128 * q, 128)
                tile = jnp.concatenate([b_ref[4 * g + m, :, lanes] for m in range(4)], axis=0)
                a[pl.ds(128 * r, 128), pl.ds(128 * q, 128)] = tile
                if q < r:
                    a[pl.ds(128 * q, 128), pl.ds(128 * r, 128)] = tile.T
    eye = (lax.broadcasted_iota(jnp.int32, (NB, NB), 0) == lax.broadcasted_iota(jnp.int32, (NB, NB), 1)).astype(f32)

    def step(kb, _):
        at = pl.ds(pl.multiple_of(kb * NB, NB), NB)
        blk = [a[pl.ds(pl.multiple_of(kb * NB + 8 * w, 8), 8), at] for w in range(NB // 8)]
        inv = pivot_inverse(blk)
        for w in range(NB // 8):
            piv[8 * w : 8 * w + 8, :] = inv[w]
        a[at, at] = eye
        u = dot3(piv[...], a[at, :])
        uh, ul = split(u)
        a[at, at] = -eye
        ch, cl = split(a[:, at])
        a[at, :] = jnp.zeros((NB, n), f32)
        a[:, at] = jnp.zeros((n, NB), f32)
        uk = jnp.concatenate([uh, ul, uh], axis=0)
        ck = jnp.concatenate([ch, ch, cl], axis=1)
        for t in range(n // 256):
            r = slice(256 * t, 256 * t + 256)
            a[r, :] = a[r, :] - dot(ck[r, :], uk)
        return 0

    lax.fori_loop(0, n // NB, step, 0)


def panel_inverse(packed):
    return pl.pallas_call(
        inverse_kernel,
        out_shape=jax.ShapeDtypeStruct((PW, PW), f32),
        in_specs=[VMEM],
        out_specs=VMEM,
        scratch_shapes=[pltpu.VMEM((NB, NB), f32)],
        compiler_params=pltpu.CompilerParams(vmem_limit_bytes=40 << 20),
        cost_estimate=pl.CostEstimate(flops=60 * 10**9, bytes_accessed=200 * 10**6, transcendentals=0),
        name="panel_inverse",
    )(packed)


def refresh_kernel(
    scale, low_ref, tok_ref, tgt_ref, res_ref, cor_ref, every, part, heard, own_low, lows,
    s_far, r_far_up, r_far_down, s_up, s_down, r_up, r_down, own,
    z_far, zr_far_up, zr_far_down, z_up, z_down, zr_up, zr_down,
    send, recv, rs_send, rs_recv, ag_send, ag_recv,
):
    i, j, zh, x, y, zl, c = place()
    x_up, x_down = (row_of(zh, x + 1), j), (row_of(zh, x + 3), j)
    z_next, z_prev = (row_of(zh + 1, x), j), (row_of(zh + 3, x), j)
    meet([(i, (j + d) % 16) for d in range(1, 16)] + [x_up, x_down, z_next, z_prev])
    copies = Copies(send, recv)
    tokens = tok_ref[...]
    half = low_ref.shape[0] // 2
    top, bottom = pl.ds(0, half), pl.ds(half, half)

    partials = []

    def use(s, block):
        value = lax.dot_general(block[...], tokens, (((1,), (1,)), ((), ())), preferred_element_type=f32)
        part[s] = value
        copy = pltpu.make_async_remote_copy(
            src_ref=part.at[s],
            dst_ref=heard.at[j],
            send_sem=rs_send.at[s],
            recv_sem=rs_recv.at[j],
            device_id=(i, s),
            device_id_type=MESH,
        )
        pl.when(s != j)(copy.start)
        partials.append((s, copy))

    def spread(s, block):
        return s, copies(block, every.at[s], x_up), copies(block, every.at[s], x_down)

    zn = copies(low_ref, every.at[i], z_next)
    zp = copies(low_ref, every.at[i], z_prev)
    sent = [spread(i, low_ref)]
    use(i, low_ref)
    zn.wait_recv()
    s = row_of(zh + 3, x)
    z1 = copies(every.at[s, top], every.at[s, top], z_next)
    sent.append(spread(s, every.at[s]))
    zp.wait_recv()
    s = row_of(zh + 1, x)
    z2 = copies(every.at[s, bottom], every.at[s, bottom], z_prev)
    sent.append(spread(s, every.at[s]))
    use(row_of(zh + 3, x), every.at[row_of(zh + 3, x)])
    use(s, every.at[s])
    z1.wait_recv()
    z2.wait_recv()
    s = row_of(zh + 2, x)
    sent.append(spread(s, every.at[s]))
    use(s, every.at[s])
    lasts = []
    for dz, (_, up, down) in zip((0, 3, 1, 2), sent):
        up.wait_recv()
        s = row_of(zh + dz, x + 3)
        a = copies(every.at[s, top], every.at[s, top], x_up)
        use(s, every.at[s])
        down.wait_recv()
        s = row_of(zh + dz, x + 1)
        b = copies(every.at[s, bottom], every.at[s, bottom], x_down)
        use(s, every.at[s])
        lasts.append((dz, a, b))
    for dz, a, b in lasts:
        a.wait_recv()
        b.wait_recv()
        s = row_of(zh + dz, x + 2)
        use(s, every.at[s])

    total = part[j] - tgt_ref[...]
    for d in range(1, 16):
        k = (j + d) % 16
        pltpu.make_async_remote_copy(
            src_ref=part.at[k],
            dst_ref=heard.at[k],
            send_sem=rs_send.at[k],
            recv_sem=rs_recv.at[k],
            device_id=(i, k),
            device_id_type=MESH,
        ).wait_recv()
        total = total + heard[k]
    res_ref[...] = total
    own_low[...] = total.astype(bf16)

    shared = []
    for d in range(1, 16):
        copy = pltpu.make_async_remote_copy(
            src_ref=own_low,
            dst_ref=lows.at[j],
            send_sem=ag_send.at[d - 1],
            recv_sem=ag_recv.at[j],
            device_id=(i, (j + d) % 16),
            device_id_type=MESH,
        )
        copy.start()
        shared.append(copy)
    lows[j] = total.astype(bf16)
    for d in range(1, 16):
        k = (j + d) % 16
        pltpu.make_async_remote_copy(
            src_ref=own_low,
            dst_ref=lows.at[k],
            send_sem=ag_send.at[d - 1],
            recv_sem=ag_recv.at[k],
            device_id=(i, k),
            device_id_type=MESH,
        ).wait_recv()

    def product(zz, xx):
        return dot(lows[row_of(zz, xx)], tokens)

    order = (2, 1, 3, 0)
    far = []
    for q, dz in enumerate(order):
        s_far[q] = product(zh + dz, x + 2).astype(bf16)
        far.append((
            copies(s_far.at[q, top], r_far_up.at[q], x_up),
            copies(s_far.at[q, bottom], r_far_down.at[q], x_down),
        ))
    near = []
    for q, dz in enumerate(order):
        value = product(zh + dz, x + 1)
        far[q][0].wait_recv()
        s_up[q, top] = (value[:half] + r_far_up[q].astype(f32)).astype(bf16)
        s_up[q, bottom] = value[half:].astype(bf16)
        a = copies(s_up.at[q], r_up.at[q], x_up)
        value = product(zh + dz, x + 3)
        far[q][1].wait_recv()
        s_down[q, top] = value[:half].astype(bf16)
        s_down[q, bottom] = (value[half:] + r_far_down[q].astype(f32)).astype(bf16)
        b = copies(s_down.at[q], r_down.at[q], x_down)
        near.append((a, b))
        own[q] = product(zh + dz, x)

    def joined(q):
        near[q][0].wait_recv()
        near[q][1].wait_recv()
        return own[q] + (r_up[q].astype(f32) + r_down[q].astype(f32))

    z_far[...] = joined(0).astype(bf16)
    za = copies(z_far.at[top], zr_far_up, z_next)
    zb = copies(z_far.at[bottom], zr_far_down, z_prev)
    value = joined(1)
    z_up[bottom] = value[half:].astype(bf16)
    za.wait_recv()
    z_up[top] = (value[:half] + zr_far_up[...].astype(f32)).astype(bf16)
    zc = copies(z_up, zr_up, z_next)
    value = joined(2)
    z_down[top] = value[:half].astype(bf16)
    zb.wait_recv()
    z_down[bottom] = (value[half:] + zr_far_down[...].astype(f32)).astype(bf16)
    zd = copies(z_down, zr_down, z_prev)
    value = joined(3)
    zc.wait_recv()
    zd.wait_recv()
    cor_ref[...] = (value + (zr_up[...].astype(f32) + zr_down[...].astype(f32))) * scale

    copies.drain()
    for s, copy in partials:
        pl.when(s != j)(copy.wait_send)
    for copy in shared:
        copy.wait_send()


def refresh(low, tokens, targets_t, scale):
    m, n = low.shape
    t = tokens.shape[0]
    sems = 4 + 16 + 16 + 4
    dma = pltpu.SemaphoreType.DMA

    def wide(*lead):
        return pltpu.VMEM((*lead, n), bf16)

    return pl.pallas_call(
        functools.partial(refresh_kernel, scale),
        out_shape=(jax.ShapeDtypeStruct((m, t), f32), jax.ShapeDtypeStruct((m, n), f32)),
        in_specs=[VMEM] * 3,
        out_specs=(VMEM, VMEM),
        scratch_shapes=[
            wide(16, m), pltpu.VMEM((16, m, t), f32), pltpu.VMEM((16, m, t), f32),
            pltpu.VMEM((m, t), bf16), pltpu.VMEM((16, m, t), bf16),
            wide(4, m), wide(4, m // 2), wide(4, m // 2), wide(4, m), wide(4, m), wide(4, m), wide(4, m),
            pltpu.VMEM((4, m, n), f32),
            wide(m), wide(m // 2), wide(m // 2), wide(m), wide(m), wide(m), wide(m),
            dma((sems,)), dma((sems,)), dma((16,)), dma((16,)), dma((15,)), dma((16,)),
        ],
        compiler_params=pltpu.CompilerParams(collective_id=1, has_side_effects=True, vmem_limit_bytes=32 << 20),
        cost_estimate=pl.CostEstimate(flops=10**9, bytes_accessed=200 * 10**6, transcendentals=0),
        name="refresh",
    )(low, tokens, targets_t)


def spread_panel(array, mine, axis):
    share = lax.psum_scatter(jnp.where(mine, array, jnp.zeros_like(array)), axis, scatter_dimension=0, tiled=True)
    return lax.all_gather(share, axis, axis=0, tiled=True)


def shards(panels, inverse, weight, tokens, targets):
    high = lax.Precision.HIGH
    i, j = lax.axis_index("row"), lax.axis_index("col")
    p = panels[0]
    packed = block_everywhere(panels, inverse)
    weight_slab = lax.psum(jnp.where(j == p, weight, jnp.zeros_like(weight)), "col")
    row_panel = spread_panel(inverse.astype(ROW_TYPE), i == p, "row").astype(f32)
    column = spread_panel(inverse.astype(COL_TYPE), j == p, "col").astype(f32)
    block_inverse = panel_inverse(packed)
    solved = jnp.dot(block_inverse, row_panel, precision=high, preferred_element_type=f32)
    pruned = weight - jnp.dot(weight_slab, solved, precision=high, preferred_element_type=f32)
    tokens_all = tokens.shape[0] * lax.axis_size("row")
    residual_t, correlation = refresh(
        pruned.astype(bf16), tokens, targets.T.astype(f32), 1.0 / math.sqrt(tokens_all)
    )
    new_inverse = inverse - jnp.dot(column, solved, precision=high, preferred_element_type=f32)
    return (new_inverse, pruned, residual_t.T, correlation)


ROW_TYPE = jnp.float32
COL_TYPE = jnp.float32


def solution(mesh):
    in_specs = (P(), P("row", "col"), P("row", "col"), P("row", "col"), P("row", "col"))
    out_specs = (P("row", "col"), P("row", "col"), P("row", "col"), P("row", "col"))
    return jax.shard_map(shards, mesh=mesh, in_specs=in_specs, out_specs=out_specs, check_vma=False)
```

time: 1030 us -> 486 us (0.47)
  waiting for transfers between devices: 508 us -> 211 us
  other arithmetic: 266 us -> 7.76 us
  Pallas kernels: 0 us -> 215 us
  local copies, waits for them, and re-layouts: 83.4 us -> 5.52 us
  matrix products: 104 us -> 27.2 us
  blocking collectives: 40.8 us -> 0 us
    another operation x33 -> x0, other arithmetic: 251 us -> none  [the longest x30 167 us: shards(): factor = jnp.linalg.cholesky(safe_block)]
    pallas_call x0 -> x3, Pallas kernels: none -> 215 us  [the longest x1 73.5 us: panel_inverse(): pl.pallas_call(inverse_kernel, out_shape=jax.ShapeDtypeStruct((PW, PW), f...]
    psum x1, waiting for transfers between devices: 203 us -> 45.8 us  [shards(): lax.psum(jnp.where(j == p, weight, jnp.zeros_like(weight)), 'col')]
    all_gather x2, waiting for transfers between devices: 102 us -> 0.02 us  [spread_panel(): return lax.all_gather(share, axis, axis=0, tiled=True)]
    another operation x44 -> x0, matrix products: 73.2 us -> none  [the longest x15 27.7 us: cholesky_apply(): lax.linalg.triangular_solve(factor, halfway, left_side=True, lower=True,...]
    all_gather x2 -> x0, blocking collectives: 40.8 us -> none  [the longest x1 21.7 us: shards(): lax.all_gather(residual.astype(jnp.bfloat16), 'col', axis=1, tiled=True)]
    another operation x77 -> x0, local copies, waits for them, and re-layouts: 40 us -> none
    reduce_scatter x3 -> x2, waiting for transfers between devices: 203 us -> 165 us  [spread_panel(): lax.psum_scatter(jnp.where(mine, array, jnp.zeros_like(array)), axis, sca...]
  transfers between devices with their start and end apart: 7 -> 5, of which waited for: 6 -> 3; matrix products, arithmetic and copies ran while one was open for 41% -> 3% of each run, Pallas kernels for 0% -> 45%
where the time goes in v1:
time: 486 us; the launch traced here: 481 us
  Pallas kernels  215 us (44%)
  waiting for transfers between devices  211 us (43%)
  matrix products  27.2 us (6%)
  between operations  14.5 us (3%)
  other arithmetic  7.76 us (2%)
  local copies, waits for them, and re-layouts  5.52 us (1%)
    reduce_scatter x2, waiting for transfers between devices, spread_panel(): lax.psum_scatter(jnp.where(mine, array, jnp.zeros_like(array)), axis, sca...  165 us
    pallas_call x1, Pallas kernels, panel_inverse(): pl.pallas_call(inverse_kernel, out_shape=jax.ShapeDtypeStruct((PW, PW), f...  73.5 us
    pallas_call x1, Pallas kernels, block_everywhere(): pl.pallas_call(block_kernel, out_shape=jax.ShapeDtypeStruct((16, PR, PC),...  72.4 us
    pallas_call x1, Pallas kernels, refresh(): pl.pallas_call(functools.partial(refresh_kernel, scale), out_shape=(jax.S...  68.9 us
    psum x1, waiting for transfers between devices, shards(): lax.psum(jnp.where(j == p, weight, jnp.zeros_like(weight)), 'col')  45.8 us
    dot_general x1, matrix products, shards(): jnp.dot(column, solved, precision=high, preferred_element_type=f32)  11.7 us
    dot_general x1, matrix products, shards(): jnp.dot(block_inverse, row_panel, precision=high, preferred_element_type=...  11.1 us
  transfers between devices with their start and end apart: 5, of which 3 were waited for; matrix products, arithmetic and copies ran while one was open for 3% of the time, Pallas kernels for 45%

profile of v1, /device:TPU:8, one launch (start us, length us, event | category | flops | bytes accessed | tf_op | source)
XLA Modules:
  0.0 481.5 jit_solution(13173171695412925601)
XLA Ops:
  7.2 0.0 reduce-scatter.5.cloned.1.call-start
  7.9 7.0 %broadcast_select_fusion = (f32[1024,1024]{1,0:T(8,128)}, f32[1024,1024]{1,0:T(8,128)}) fusion(f32[1024,1024]{1,0:T(8,128)} %h_ref.1, pred[]{:T(512)S(6)} %eq.8, pred[]{:T(512)S(6)} %eq.7), kind=kLoop, calls=%fused_computation | loop fusion | flops 2097152 | bytes 12582914 | tf_op jit(solution)/shard_map/jit(_where)/select_n | solution.py:479
  14.9 0.0 reduce-scatter.5.cloned.1.call-update
  14.9 0.0 reduce-scatter.3.cloned.1.call-start
  15.0 0.7 reduce-scatter.3.cloned.1.call-update
  15.7 0.0 copy-start.4
  15.7 0.0 all-gather.5.cloned.1.call-start
  15.7 99.5 %reduce-scatter.5.cloned.1.call-done = f32[64,1024]{1,0:T(8,128)} async-done(((f32[1024,1024]{1,0:T(8,128)}), f32[64,1024]{1,0:T(8,128)}) %reduce-scatter.5.cloned.1.call-update) | async-done | bytes 262160 | tf_op jit(solution)/shard_map/reduce_scatter | solution.py:479
  115.2 0.0 all-gather.5.cloned.1.call-update
  115.2 0.0 all-reduce.2.cloned.1.call-start
  115.3 0.0 copy-done.3
  115.3 0.7 broadcast_select_fusion.2
  116.0 0.0 all-reduce.2.cloned.1.call-update
  116.0 0.0 all-gather.3.cloned.1.call-start
  116.1 65.3 %reduce-scatter.3.cloned.1.call-done = f32[64,1024]{1,0:T(8,128)} async-done(((f32[1024,1024]{1,0:T(8,128)}), f32[64,1024]{1,0:T(8,128)}) %reduce-scatter.3.cloned.1.call-update) | async-done | bytes 262160 | tf_op jit(solution)/shard_map/reduce_scatter | solution.py:479
  181.4 0.0 all-gather.3.cloned.1.call-update
  181.4 0.0 copy-start
  181.5 2.2 copy-done
  183.6 72.4 %block_everywhere.1.b_ref = f32[16,32,1152]{2,1,0:T(8,128)S(1)} custom-call(s32[1]{0:T(128)} %copy.12.p_ref, f32[1024,1024]{1,0:T(8,128)S(1)} %copy-done), custom_call_target="tpu_custom_call" | custom-call | flops 1000000000 | bytes 160000000 | tf_op jit(solution)/shard_map/block_everywhere/pallas_call | solution.py:172
  256.1 0.0 copy-done.4
  256.1 73.5 %panel_inverse.1 = f32[1024,1024]{1,0:T(8,128)S(1)} custom-call(f32[16,32,1152]{2,1,0:T(8,128)S(1)} %block_everywhere.1.b_ref), custom_call_target="tpu_custom_call" | custom-call | flops 60000002048 | bytes 200000000 | tf_op jit(solution)/shard_map/panel_inverse/pallas_call | solution.py:273
  329.7 0.0 copy-start.2
  329.7 2.0 copy-done.2
  331.7 11.1 %fusion.1 = f32[1024,1024]{1,0:T(8,128)} fusion(f32[1024,1024]{1,0:T(8,128)} %copy-done.2, f32[1024,1024]{1,0:T(8,128)} %all-gather.5.cloned.1.call-done), kind=kOutput, calls=%fused_computation.7 | convolution fusion | flops 6442450944 | bytes 12582912 | tf_op jit(solution)/shard_map/dot_general | solution.py:492
  342.8 45.8 %all-reduce.2.cloned.1.call-done = f32[64,1024]{1,0:T(8,128)} async-done(((f32[64,1024]{1,0:T(8,128)}), f32[64,1024]{1,0:T(8,128)}) %all-reduce.2.cloned.1.call-update) | async-done | bytes 262160 | tf_op jit(solution)/shard_map/psum | solution.py:488
  388.6 4.4 fusion
  393.0 0.0 copy-done.1
  393.0 68.9 %refresh.1 = (f32[64,128]{1,0:T(8,128)S(1)}, f32[64,1024]{1,0:T(8,128)S(1)}) custom-call(bf16[64,1024]{1,0:T(8,128)(2,1)S(1)} %get-tuple-element.10.low_ref, bf16[128,1024]{1,0:T(8,128)(2,1)S(1)} %copy-done.1, f32[64,128]{1,0:T(8,128)S(1)} %convert_bitcast_fusion.tgt_ref), custom_call_target="tpu_custom_call" | custom-call | flops 1000000000 | bytes 200000000 | tf_op jit(solution)/shard_map/refresh/pallas_call | solution.py:459
  461.9 0.0 all-gather.3.cloned.1.call-done
  461.9 11.7 %convolution_subtract_fusion = f32[1024,1024]{1,0:T(8,128)} fusion(f32[1024,1024]{1,0:T(8,128)} %h_ref.1, f32[1024,1024]{1,0:T(8,128)} %all-gather.3.cloned.1.call-done, f32[1024,1024]{1,0:T(8,128)} %fusion.1), kind=kOutput, calls=%fused_computation.2 | convolution fusion | flops 6443499520 | bytes 16777216 | tf_op jit(solution)/shard_map/dot_general | solution.py:498
  473.7 0.6 copy.13
  474.3 0.7 copy.14
  (4 shorter events, 0.0 us)
Async XLA Ops:
  7.2 108.0 %reduce-scatter.5.cloned.1.call-start = ((), (), s32[]{:S(2)}) async-start(), calls=%async_computation.4 | async-start | bytes 4456448 | tf_op jit(solution)/shard_map/reduce_scatter | solution.py:479
  14.9 100.4 %copy-start.3 = (f32[64,1024]{1,0:T(8,128)S(1)}, f32[64,1024]{1,0:T(8,128)}, u32[]{:S(2)}) copy-start(f32[64,1024]{1,0:T(8,128)} %param.7) | copy-start | bytes 786436
  14.9 166.5 %reduce-scatter.3.cloned.1.call-start = ((), (), s32[]{:S(2)}) async-start(), calls=%async_computation.2 | async-start | bytes 4456448 | tf_op jit(solution)/shard_map/reduce_scatter | solution.py:479
  15.7 240.4 %copy-start.4 = (bf16[128,64]{0,1:T(8,128)(2,1)S(1)}, bf16[128,64]{0,1:T(8,128)(2,1)}, u32[]{:S(2)}) copy-start(bf16[128,64]{0,1:T(8,128)(2,1)} %param.9) | copy-start | bytes 49156
  15.7 316.0 %all-gather.5.cloned.1.call-start = ((), (), s32[]{:S(2)}) async-start(), calls=%async_computation.5 | async-start | bytes 4456448 | tf_op jit(solution)/shard_map/all_gather | solution.py:480
  115.2 273.4 %all-reduce.2.cloned.1.call-start = ((), (), s32[]{:S(2)}) async-start(), calls=%async_computation.6 | async-start | bytes 524288 | tf_op jit(solution)/shard_map/psum | solution.py:488
  116.0 345.9 %all-gather.3.cloned.1.call-start = ((), (), s32[]{:S(2)}) async-start(), calls=%async_computation.3 | async-start | bytes 4456448 | tf_op jit(solution)/shard_map/all_gather | solution.py:480
  181.4 2.2 copy-start
  329.7 2.0 copy-start.2
  342.8 50.2 %copy-start.1 = (bf16[128,1024]{1,0:T(8,128)(2,1)S(1)}, bf16[128,1024]{1,0:T(8,128)(2,1)}, u32[]{:S(2)}) copy-start(bf16[128,1024]{1,0:T(8,128)(2,1)} %tok_ref.1) | copy-start | bytes 786436
Sparse Core Ops, SparseCore 0:
  15.0 100.1 reduce-scatter.4
  117.7 63.6 reduce-scatter.2
  183.9 79.3 all-gather.4
  266.3 122.2 all-reduce.1
  390.3 54.0 all-gather.2

commit v2 on v1

--- a/solution.py
+++ b/solution.py
@@ -33,7 +33,7 @@
     def __init__(self, send, recv):
         self.send, self.recv, self.made = send, recv, []
 
-    def __call__(self, src, dst, device):
+    def plan(self, src, dst, device):
         n = len(self.made)
         copy = pltpu.make_async_remote_copy(
             src_ref=src,
@@ -43,8 +43,12 @@
             device_id=device,
             device_id_type=MESH,
         )
+        self.made.append(copy)
+        return copy
+
+    def __call__(self, src, dst, device):
+        copy = self.plan(src, dst, device)
         copy.start()
-        self.made.append(copy)
         return copy
 
     def drain(self):
@@ -60,18 +64,47 @@
 
 
 PR, PC = 32, 1152
-
-
-def block_kernel(p_ref, h_ref, out_ref, pack, chunk, got, mine, zgot, local, send1, recv1, send, recv):
+CB = 136
+CT = 72
+
+
+def at(start, size):
+    return pl.ds(pl.multiple_of(start, 8), size)
+
+
+def fill(dst, start, rows, value):
+    @pl.loop(0, rows // 8)
+    def _(t):
+        r = pl.multiple_of(t * 8, 8)
+        dst[at(start + r, 8), :] = value(r)
+
+
+def front_kernel(
+    p_ref, h_ref, w_ref, a, rows, cw, pruned_ref, low_ref,
+    hw, pack, chunk, got, mine, zgot, packed, piv,
+    ra, sb, rb, acc, rz, sz, rzn,
+    rc, m0, ryu, ryd, sy, ry, acc_c, rcz,
+    local, send1, recv1, send, recv,
+):
     i, j, zh, x, y, zl, c = place()
     p = p_ref[0]
+    loads = [
+        pltpu.make_async_copy(h_ref, hw.at[pl.ds(0, PW)], local.at[9]),
+        pltpu.make_async_copy(w_ref, hw.at[pl.ds(PW, 64)], local.at[10]),
+    ]
+    for load in loads:
+        load.start()
     xs = [(row_of(zh, x + d), j) for d in (1, 2, 3)]
     zs = [(row_of(zh + d, x), j) for d in (1, 2, 3)]
     meet([(i, (j + d) % 16) for d in range(1, 16)] + xs + zs)
+    x_up, x_down, z_next, z_prev = xs[0], xs[2], zs[0], zs[2]
+    y_up, y_down = (i, col_of(y + 1, zl, c)), (i, col_of(y + 3, zl, c))
+    across, peer = (i, col_of(y, zl + 1, c)), (i, col_of(y, zl, c + 1))
+    copies = Copies(send, recv)
 
     scatter = [
         pltpu.make_async_remote_copy(
-            src_ref=pack.at[pl.ds(pl.multiple_of(((j + d) % 16) * PR, PR), PR)],
+            src_ref=pack.at[at(((j + d) % 16) * PR, PR)],
             dst_ref=chunk,
             send_sem=send1.at[d - 1],
             recv_sem=recv1,
@@ -85,52 +118,272 @@
     def _():
         loads = []
         for g in range(4):
-            rows = pl.ds(128 * g, 128)
-            a, b = 128 * (g + 1), 128 * (8 - g)
-            loads.append(pltpu.make_async_copy(h_ref.at[rows, pl.ds(0, a)], pack.at[rows, pl.ds(0, a)], local.at[2 * g]))
+            r = pl.ds(128 * g, 128)
+            m, n = 128 * (g + 1), 128 * (8 - g)
+            loads.append(pltpu.make_async_copy(h_ref.at[r, pl.ds(0, m)], pack.at[r, pl.ds(0, m)], local.at[2 * g]))
             far = pl.ds(128 * (7 - g), 128)
-            loads.append(pltpu.make_async_copy(h_ref.at[far, pl.ds(0, b)], pack.at[rows, pl.ds(a, b)], local.at[2 * g + 1]))
+            loads.append(pltpu.make_async_copy(h_ref.at[far, pl.ds(0, n)], pack.at[r, pl.ds(m, n)], local.at[2 * g + 1]))
         for load in loads:
             load.start()
         for load in loads:
             load.wait()
         for copy in scatter:
             copy.start()
-        own = pltpu.make_async_copy(pack.at[pl.ds(pl.multiple_of(j * PR, PR), PR)], chunk, local.at[8])
+        own = pltpu.make_async_copy(pack.at[at(j * PR, PR)], chunk, local.at[8])
         own.start()
         own.wait()
+
+    for load in loads:
+        load.wait()
+
+    own_row = i == p
+    far = ((x + 2) % 4) * 256
+    ra_up = copies(hw.at[at(far, 128)], ra.at[0], x_up)
+    ra_down = copies(hw.at[at(far + 128, 128)], ra.at[1], x_down)
+    rb_up = copies.plan(sb.at[0], rb.at[0], x_up)
+    rb_down = copies.plan(sb.at[1], rb.at[1], x_down)
+    far = ((zh + 2) % 4) * 64
+    za_up = copies.plan(acc.at[at(far, 32)], rz.at[0], z_next)
+    za_down = copies.plan(acc.at[at(far + 32, 32)], rz.at[1], z_prev)
+    zb_up = copies.plan(sz.at[0], rzn.at[0], z_next)
+    zb_down = copies.plan(sz.at[1], rzn.at[1], z_prev)
+
+    def chunk_at(k):
+        return x * 256 + ((zh + k) % 4) * 64
+
+    def block_at(k):
+        return ((x + k) % 4) * 256
+
+    def same(ref, start, size, device):
+        return copies.plan(ref.at[at(start, size)], ref.at[at(start, size)], device)
+
+    ga = [same(rows, chunk_at(0), 64, z_next), same(rows, chunk_at(0), 64, z_prev)]
+    gb = [same(rows, chunk_at(3), 32, z_next), same(rows, chunk_at(1) + 32, 32, z_prev)]
+    gx = [same(rows, block_at(0), 256, x_up), same(rows, block_at(0), 256, x_down)]
+    gy = [same(rows, block_at(3), 128, x_up), same(rows, block_at(1) + 128, 128, x_down)]
+
+    def held(r):
+        return jnp.where(own_row, hw[at(r, 8), :], 0.0)
+
+    def rows_near():
+        ra_up.wait_recv()
+        ra_down.wait_recv()
+        before = row_of(zh, x + 3) == p
+        after = row_of(zh, x + 1) == p
+        up, down = block_at(1), block_at(3)
+        fill(sb.at[0], 0, 128, lambda r: held(up + r) + jnp.where(before, ra[0, at(r, 8), :], 0.0))
+        fill(sb.at[0], 128, 128, lambda r: held(up + 128 + r))
+        rb_up.start()
+        fill(sb.at[1], 0, 128, lambda r: held(down + r))
+        fill(sb.at[1], 128, 128, lambda r: held(down + 128 + r) + jnp.where(after, ra[1, at(r, 8), :], 0.0))
+        rb_down.start()
+
+    def rows_z_far():
+        rb_up.wait_recv()
+        rb_down.wait_recv()
+        fill(acc, 0, 256, lambda r: held(block_at(0) + r) + (rb[0, at(r, 8), :] + rb[1, at(r, 8), :]))
+        za_up.start()
+        za_down.start()
+
+    def rows_z_near():
+        za_up.wait_recv()
+        za_down.wait_recv()
+        up, down = ((zh + 1) % 4) * 64, ((zh + 3) % 4) * 64
+        fill(sz.at[0], 0, 32, lambda r: acc[at(up + r, 8), :] + rz[0, at(r, 8), :])
+        fill(sz.at[0], 32, 32, lambda r: acc[at(up + 32 + r, 8), :])
+        zb_up.start()
+        fill(sz.at[1], 0, 32, lambda r: acc[at(down + r, 8), :])
+        fill(sz.at[1], 32, 32, lambda r: acc[at(down + 32 + r, 8), :] + rz[1, at(r, 8), :])
+        zb_down.start()
+
+    def rows_final():
+        zb_up.wait_recv()
+        zb_down.wait_recv()
+        mid = zh * 64
+        fill(rows, chunk_at(0), 64, lambda r: acc[at(mid + r, 8), :] + (rzn[0, at(r, 8), :] + rzn[1, at(r, 8), :]))
+        for copy in ga:
+            copy.start()
+
+    def handed(waits, starts):
+        for copy in waits:
+            copy.wait_recv()
+        for copy in starts:
+            copy.start()
+
+    ca = copies(hw.at[at((1 - c) * 4 * CB, 4 * CB)], rc, peer)
+    far = ((y + 2) % 4) * CB
+    ya_up = copies.plan(m0.at[at(far, CT)], ryu, y_up)
+    ya_down = copies.plan(m0.at[at(far + CT, CB - CT)], ryd, y_down)
+    yb_up = copies.plan(sy.at[0], ry.at[0], y_up)
+    yb_down = copies.plan(sy.at[1], ry.at[1], y_down)
+    cz = copies.plan(acc_c, rcz, across)
+
+    def col_at(k):
+        return c * 4 * CB + ((y + k) % 4) * CB
+
+    cy = [same(cw, col_at(0), CB, y_up), same(cw, col_at(0), CB, y_down)]
+    cy2 = [same(cw, col_at(3), CT, y_up), same(cw, col_at(1) + CT, CB - CT, y_down)]
+    cc = [same(cw, col_at(k), CB, peer) for k in range(4)]
+
+    def cols_far():
+        ca.wait_recv()
+        own, other = j == p, col_of(y, zl, c + 1) == p
+        base = c * 4 * CB
+        fill(m0, 0, 4 * CB, lambda r: jnp.where(own, hw[at(base + r, 8), :], 0.0) + jnp.where(other, rc[at(r, 8), :], 0.0))
+        ya_up.start()
+        ya_down.start()
+
+    def cols_near():
+        ya_up.wait_recv()
+        ya_down.wait_recv()
+        up, down = ((y + 1) % 4) * CB, ((y + 3) % 4) * CB
+        fill(sy.at[0], 0, CT, lambda r: m0[at(up + r, 8), :] + ryu[at(r, 8), :])
+        fill(sy.at[0], CT, CB - CT, lambda r: m0[at(up + CT + r, 8), :])
+        yb_up.start()
+        fill(sy.at[1], 0, CT, lambda r: m0[at(down + r, 8), :])
+        fill(sy.at[1], CT, CB - CT, lambda r: m0[at(down + CT + r, 8), :] + ryd[at(r, 8), :])
+        yb_down.start()
+
+    def cols_across():
+        yb_up.wait_recv()
+        yb_down.wait_recv()
+        mid = y * CB
+        fill(acc_c, 0, CB, lambda r: m0[at(mid + r, 8), :] + (ry[0, at(r, 8), :] + ry[1, at(r, 8), :]))
+        cz.start()
+
+    def cols_final():
+        cz.wait_recv()
+        fill(cw, col_at(0), CB, lambda r: acc_c[at(r, 8), :] + rcz[at(r, 8), :])
+        for copy in cy + cc[:1]:
+            copy.start()
 
     @pl.when(i != j)
     def _():
         scatter[0].wait_recv()
 
-    copies = Copies(send, recv)
-
     def piece(k):
-        return pl.ds(pl.multiple_of((k % 4) * 8, 8), 8)
+        return at((k % 4) * 8, 8)
 
     firsts = [copies(chunk.at[piece(x + d)], got.at[d - 1], xs[d - 1]) for d in (1, 2, 3)]
-    held = jnp.where(i == p, chunk[piece(x), :], 0.0)
+    part = jnp.where(own_row, chunk[piece(x), :], 0.0)
     for d in (1, 2, 3):
         firsts[d - 1].wait_recv()
-        held = held + jnp.where(row_of(zh, x - d + 4) == p, got[d - 1], 0.0)
-    mine[...] = held
+        part = part + jnp.where(row_of(zh, x - d + 4) == p, got[d - 1], 0.0)
+    mine[...] = part
     seconds = [copies(mine, zgot.at[d - 1], zs[d - 1]) for d in (1, 2, 3)]
     for d in (1, 2, 3):
         seconds[d - 1].wait_recv()
-        held = held + zgot[d - 1]
-    out_ref[j, piece(x), :] = held
-    thirds = [copies(out_ref.at[j, piece(x)], out_ref.at[j, piece(x)], xs[d - 1]) for d in (1, 2, 3)]
+        part = part + zgot[d - 1]
+    packed[j, piece(x), :] = part
+    thirds = [copies(packed.at[j, piece(x)], packed.at[j, piece(x)], xs[d - 1]) for d in (1, 2, 3)]
     for copy in thirds:
         copy.wait_recv()
-
-    gather_cols(copies, out_ref, out_ref, PR)
+    rows_near()
+    gather_cols(copies, packed, packed, PR)
+
+    stages = [
+        (rows_z_far, cols_far),
+        (rows_z_near, cols_near),
+        (rows_final, cols_across),
+        (lambda: handed(ga, gb), cols_final),
+        (lambda: handed(gb, gx), lambda: handed(cy, cy2 + [cc[3], cc[1]])),
+        (lambda: handed(cy2, [cc[2]]),),
+        (lambda: handed(gx, gy),),
+        (lambda: handed(cc, []),),
+    ]
+
+    for g in range(4):
+        for r, start in ((g, 0), (7 - g, 128 * (g + 1))):
+            for q in range(r + 1):
+                lanes = pl.ds(start + 128 * q, 128)
+                tile = jnp.concatenate([packed[4 * g + m, :, lanes] for m in range(4)], axis=0)
+                a[pl.ds(128 * r, 128), pl.ds(128 * q, 128)] = tile
+                if q < r:
+                    a[pl.ds(128 * q, 128), pl.ds(128 * r, 128)] = tile.T
+    eye = (lax.broadcasted_iota(jnp.int32, (NB, NB), 0) == lax.broadcasted_iota(jnp.int32, (NB, NB), 1)).astype(f32)
+
+    def step(kb, _):
+        for n, stage in enumerate(stages):
+
+            @pl.when(kb == n)
+            def _():
+                for part in stage:
+                    part()
+
+        sweep(a, piv, eye, kb)
+        return 0
+
+    lax.fori_loop(0, PW // NB, step, 0)
+    handed(gy, [])
+
+    lead = dot3(cw[pl.ds(PW, 64), :], a[...])
+    for t in range(4):
+        lanes = pl.ds(256 * t, 256)
+        value = hw[pl.ds(PW, 64), lanes] - dot3(lead, rows[:, lanes])
+        pruned_ref[:, lanes] = value
+        low_ref[:, lanes] = value.astype(bf16)
+
     copies.drain()
 
     @pl.when(i == j)
     def _():
         for copy in scatter:
             copy.wait_send()
+
+
+def sweep(a, piv, eye, kb):
+    n = PW
+    here = pl.ds(pl.multiple_of(kb * NB, NB), NB)
+    blk = [a[pl.ds(pl.multiple_of(kb * NB + 8 * w, 8), 8), here] for w in range(NB // 8)]
+    inv = pivot_inverse(blk)
+    for w in range(NB // 8):
+        piv[8 * w : 8 * w + 8, :] = inv[w]
+    a[here, here] = eye
+    u = dot3(piv[...], a[here, :])
+    uh, ul = split(u)
+    a[here, here] = -eye
+    ch, cl = split(a[:, here])
+    a[here, :] = jnp.zeros((NB, n), f32)
+    a[:, here] = jnp.zeros((n, NB), f32)
+    uk = jnp.concatenate([uh, ul, uh], axis=0)
+    ck = jnp.concatenate([ch, ch, cl], axis=1)
+    for t in range(n // 256):
+        r = slice(256 * t, 256 * t + 256)
+        a[r, :] = a[r, :] - dot(ck[r, :], uk)
+
+
+def front(panels, inverse, weight):
+    sems = 9 + 25 + 16 + 14
+    dma = pltpu.SemaphoreType.DMA
+
+    def buf(*shape):
+        return pltpu.VMEM((*shape, PW), f32)
+
+    def out(*shape):
+        return jax.ShapeDtypeStruct(shape, f32)
+
+    return pl.pallas_call(
+        front_kernel,
+        out_shape=(out(PW, PW), out(PW, PW), out(8 * CB, PW), out(64, PW), jax.ShapeDtypeStruct((64, PW), bf16)),
+        in_specs=[pl.BlockSpec(memory_space=pltpu.SMEM)] + [pl.BlockSpec(memory_space=pl.ANY)] * 2,
+        out_specs=(VMEM,) * 5,
+        scratch_shapes=[
+            buf(8 * CB),
+            pltpu.VMEM((16 * PR, PC), f32),
+            pltpu.VMEM((PR, PC), f32),
+            pltpu.VMEM((3, 8, PC), f32),
+            pltpu.VMEM((8, PC), f32),
+            pltpu.VMEM((3, 8, PC), f32),
+            pltpu.VMEM((16, PR, PC), f32),
+            pltpu.VMEM((NB, NB), f32),
+            buf(2, 128), buf(2, 256), buf(2, 256), buf(256), buf(2, 32), buf(2, 64), buf(2, 64),
+            buf(4 * CB), buf(4 * CB), buf(CT), buf(CB - CT), buf(2, CB), buf(2, CB), buf(CB), buf(CB),
+            dma((11,)), dma((15,)), dma, dma((sems,)), dma((sems,)),
+        ],
+        compiler_params=pltpu.CompilerParams(collective_id=0, has_side_effects=True, vmem_limit_bytes=60 << 20),
+        cost_estimate=pl.CostEstimate(flops=60 * 10**9, bytes_accessed=400 * 10**6, transcendentals=0),
+        name="front",
+    )(panels, inverse, weight)
 
 
 def gather_cols(copies, first, out, rows):
@@ -167,31 +420,6 @@
         copy.wait_recv()
 
 
-def block_everywhere(panels, inverse):
-    sems = 9 + 25
-    return pl.pallas_call(
-        block_kernel,
-        out_shape=jax.ShapeDtypeStruct((16, PR, PC), f32),
-        in_specs=[pl.BlockSpec(memory_space=pltpu.SMEM), pl.BlockSpec(memory_space=pl.ANY)],
-        out_specs=VMEM,
-        scratch_shapes=[
-            pltpu.VMEM((16 * PR, PC), f32),
-            pltpu.VMEM((PR, PC), f32),
-            pltpu.VMEM((3, 8, PC), f32),
-            pltpu.VMEM((8, PC), f32),
-            pltpu.VMEM((3, 8, PC), f32),
-            pltpu.SemaphoreType.DMA((9,)),
-            pltpu.SemaphoreType.DMA((15,)),
-            pltpu.SemaphoreType.DMA,
-            pltpu.SemaphoreType.DMA((sems,)),
-            pltpu.SemaphoreType.DMA((sems,)),
-        ],
-        compiler_params=pltpu.CompilerParams(collective_id=0, has_side_effects=True, vmem_limit_bytes=24 << 20),
-        cost_estimate=pl.CostEstimate(flops=10**9, bytes_accessed=160 * 10**6, transcendentals=0),
-        name="block_everywhere",
-    )(panels, inverse)
-
-
 def split(x):
     hi = x.astype(bf16)
     return hi, (x - hi.astype(f32)).astype(bf16)
@@ -232,54 +460,6 @@
                 base = jnp.where(sub == s, u0, jnp.where(sub == s + 1, u1, base))
             rows[w] = base
     return rows
-
-
-def inverse_kernel(b_ref, a, piv):
-    n = PW
-    for g in range(4):
-        for r, start in ((g, 0), (7 - g, 128 * (g + 1))):
-            for q in range(r + 1):
-                lanes = pl.ds(start + 128 * q, 128)
-                tile = jnp.concatenate([b_ref[4 * g + m, :, lanes] for m in range(4)], axis=0)
-                a[pl.ds(128 * r, 128), pl.ds(128 * q, 128)] = tile
-                if q < r:
-                    a[pl.ds(128 * q, 128), pl.ds(128 * r, 128)] = tile.T
-    eye = (lax.broadcasted_iota(jnp.int32, (NB, NB), 0) == lax.broadcasted_iota(jnp.int32, (NB, NB), 1)).astype(f32)
-
-    def step(kb, _):
-        at = pl.ds(pl.multiple_of(kb * NB, NB), NB)
-        blk = [a[pl.ds(pl.multiple_of(kb * NB + 8 * w, 8), 8), at] for w in range(NB // 8)]
-        inv = pivot_inverse(blk)
-        for w in range(NB // 8):
-            piv[8 * w : 8 * w + 8, :] = inv[w]
-        a[at, at] = eye
-        u = dot3(piv[...], a[at, :])
-        uh, ul = split(u)
-        a[at, at] = -eye
-        ch, cl = split(a[:, at])
-        a[at, :] = jnp.zeros((NB, n), f32)
-        a[:, at] = jnp.zeros((n, NB), f32)
-        uk = jnp.concatenate([uh, ul, uh], axis=0)
-        ck = jnp.concatenate([ch, ch, cl], axis=1)
-        for t in range(n // 256):
-            r = slice(256 * t, 256 * t + 256)
-            a[r, :] = a[r, :] - dot(ck[r, :], uk)
-        return 0
-
-    lax.fori_loop(0, n // NB, step, 0)
-
-
-def panel_inverse(packed):
-    return pl.pallas_call(
-        inverse_kernel,
-        out_shape=jax.ShapeDtypeStruct((PW, PW), f32),
-        in_specs=[VMEM],
-        out_specs=VMEM,
-        scratch_shapes=[pltpu.VMEM((NB, NB), f32)],
-        compiler_params=pltpu.CompilerParams(vmem_limit_bytes=40 << 20),
-        cost_estimate=pl.CostEstimate(flops=60 * 10**9, bytes_accessed=200 * 10**6, transcendentals=0),
-        name="panel_inverse",
-    )(packed)
 
 
 def refresh_kernel(
@@ -475,32 +655,14 @@
     )(low, tokens, targets_t)
 
 
-def spread_panel(array, mine, axis):
-    share = lax.psum_scatter(jnp.where(mine, array, jnp.zeros_like(array)), axis, scatter_dimension=0, tiled=True)
-    return lax.all_gather(share, axis, axis=0, tiled=True)
-
-
 def shards(panels, inverse, weight, tokens, targets):
     high = lax.Precision.HIGH
-    i, j = lax.axis_index("row"), lax.axis_index("col")
-    p = panels[0]
-    packed = block_everywhere(panels, inverse)
-    weight_slab = lax.psum(jnp.where(j == p, weight, jnp.zeros_like(weight)), "col")
-    row_panel = spread_panel(inverse.astype(ROW_TYPE), i == p, "row").astype(f32)
-    column = spread_panel(inverse.astype(COL_TYPE), j == p, "col").astype(f32)
-    block_inverse = panel_inverse(packed)
+    block_inverse, row_panel, columns, pruned, low = front(panels, inverse, weight)
+    token_count = tokens.shape[0] * lax.axis_size("row")
+    residual_t, correlation = refresh(low, tokens, targets.T.astype(f32), 1.0 / math.sqrt(token_count))
     solved = jnp.dot(block_inverse, row_panel, precision=high, preferred_element_type=f32)
-    pruned = weight - jnp.dot(weight_slab, solved, precision=high, preferred_element_type=f32)
-    tokens_all = tokens.shape[0] * lax.axis_size("row")
-    residual_t, correlation = refresh(
-        pruned.astype(bf16), tokens, targets.T.astype(f32), 1.0 / math.sqrt(tokens_all)
-    )
-    new_inverse = inverse - jnp.dot(column, solved, precision=high, preferred_element_type=f32)
+    new_inverse = inverse - jnp.dot(columns[:PW], solved, precision=high, preferred_element_type=f32)
     return (new_inverse, pruned, residual_t.T, correlation)
-
-
-ROW_TYPE = jnp.float32
-COL_TYPE = jnp.float32
 
 
 def solution(mesh):

time: 486 us -> 258 us (0.53)
  waiting for transfers between devices: 211 us -> 0 us
  Pallas kernels: 215 us -> 235 us
  between operations: 14.5 us -> 1.38 us
  matrix products: 27.2 us -> 18.9 us
  other arithmetic: 7.76 us -> 0.01 us
    reduce_scatter x2 -> x0, waiting for transfers between devices: 165 us -> none  [spread_panel(): lax.psum_scatter(jnp.where(mine, array, jnp.zeros_like(array)), axis, sca...]
    psum x1 -> x0, waiting for transfers between devices: 45.8 us -> none  [shards(): lax.psum(jnp.where(j == p, weight, jnp.zeros_like(weight)), 'col')]
    pallas_call x2 -> x1, Pallas kernels: 146 us -> 168 us  [front(): pl.pallas_call(front_kernel, out_shape=(out(PW, PW), out(PW, PW), out(8 *...]
    dot_general x2 -> x1, matrix products: 16.1 us -> 8.21 us  [shards(): jnp.dot(columns[:PW], solved, precision=high, preferred_element_type=f32)]
    select_n x2 -> x0, other arithmetic: 7.75 us -> none  [the longest x1 7.03 us: spread_panel(): jnp.where(mine, array, jnp.zeros_like(array))]
  transfers between devices with their start and end apart: 5 -> 0, of which waited for: 3 -> 0; matrix products, arithmetic and copies ran while one was open for 3% -> 0% of each run, Pallas kernels for 45% -> 0%
where the time goes in v2:
time: 258 us
  Pallas kernels  235 us (91%)
  matrix products  18.9 us (7%)
    pallas_call x1, Pallas kernels, front(): pl.pallas_call(front_kernel, out_shape=(out(PW, PW), out(PW, PW), out(8 *...  168 us
    pallas_call x1, Pallas kernels, refresh(): pl.pallas_call(functools.partial(refresh_kernel, scale), out_shape=(jax.S...  67.5 us
    dot_general x1, matrix products, shards(): jnp.dot(block_inverse, row_panel, precision=high, preferred_element_type=...  10.7 us
    dot_general x1, matrix products, shards(): jnp.dot(columns[:PW], solved, precision=high, preferred_element_type=f32)  8.21 us

profile of v2, /device:TPU:8, one launch (start us, length us, event | category | flops | bytes accessed | tf_op | source)
XLA Modules:
  0.0 257.6 jit_solution(12034709112577630717)
XLA Ops:
  1.3 167.7 %front.1 = (f32[1024,1024]{1,0:T(8,128)}, f32[1024,1024]{1,0:T(8,128)}, f32[1088,1024]{1,0:T(8,128)}, f32[64,1024]{1,0:T(8,128)}, bf16[64,1024]{1,0:T(8,128)(2,1)}) custom-call(s32[1]{0:T(128)S(6)} %copy.12.p_ref, f32[1024,1024]{1,0:T(8,128)} %h_ref.1, f32[64,1024]{1,0:T(8,128)} %w_ref.1), custom_call_target="tpu_custom_call" | custom-call | flops 60000002048 | bytes 400000000 | tf_op jit(solution)/shard_map/front/pallas_call | solution.py:365
  169.0 0.0 copy-start.2
  169.0 0.0 copy-start.3
  169.0 10.7 %fusion.5 = f32[1024,1024]{1,0:T(8,128)S(1)} fusion(f32[1024,1024]{1,0:T(8,128)} %get-tuple-element.12, f32[1024,1024]{1,0:T(8,128)} %get-tuple-element.13), kind=kOutput, calls=%fused_computation.4 | convolution fusion | flops 6442450944 | bytes 12582912 | tf_op jit(solution)/shard_map/dot_general | solution.py:663
  179.7 0.0 copy-done.2
  179.7 0.0 copy-done.3
  179.7 0.0 copy-start.5
  179.8 0.0 copy-start
  179.8 0.0 copy-start.1
  179.8 0.0 copy-start.4
  179.8 8.2 %fusion.2 = f32[1024,1024]{1,0:T(8,128)} fusion(f32[1024,1024]{1,0:T(8,128)S(1)} %copy-done.2, f32[1024,1024]{1,0:T(8,128)S(1)} %fusion.5, f32[1088,1024]{1,0:T(8,128)S(1)} %copy-done.3), kind=kOutput, calls=%fused_computation.2 | convolution fusion | flops 6443499520 | bytes 16777216 | tf_op jit(solution)/shard_map/dot_general | solution.py:664
  188.0 0.0 copy-done.5
  188.0 0.0 copy-done
  188.0 0.0 copy-done.1
  188.0 67.5 %refresh.1 = (f32[64,128]{1,0:T(8,128)S(1)}, f32[64,1024]{1,0:T(8,128)S(1)}) custom-call(bf16[64,1024]{1,0:T(8,128)(2,1)S(1)} %copy-done.1, bf16[128,1024]{1,0:T(8,128)(2,1)S(1)} %copy-done, f32[64,128]{1,0:T(8,128)S(1)} %convert_bitcast_fusion.tgt_ref), custom_call_target="tpu_custom_call" | custom-call | flops 1000000000 | bytes 200000000 | tf_op jit(solution)/shard_map/refresh/pallas_call | solution.py:639
  255.6 0.0 copy-done.4
  255.6 0.7 copy.13
  256.3 0.6 copy.14
  256.9 0.7 copy.15
  (1 shorter events, 0.0 us)
Async XLA Ops:
  169.0 10.8 %copy-start.2 = (f32[1024,1024]{1,0:T(8,128)S(1)}, f32[1024,1024]{1,0:T(8,128)}, u32[]{:S(2)}) copy-start(f32[1024,1024]{1,0:T(8,128)} %h_ref.1) | copy-start | bytes 12582916
  169.0 10.8 %copy-start.3 = (f32[1088,1024]{1,0:T(8,128)S(1)}, f32[1088,1024]{1,0:T(8,128)}, u32[]{:S(2)}) copy-start(f32[1088,1024]{1,0:T(8,128)} %get-tuple-element.11) | copy-start | bytes 13369348
  179.7 8.3 %copy-start.5 = (bf16[128,64]{0,1:T(8,128)(2,1)S(1)}, bf16[128,64]{0,1:T(8,128)(2,1)}, u32[]{:S(2)}) copy-start(bf16[128,64]{0,1:T(8,128)(2,1)} %param.9) | copy-start | bytes 49156
  179.8 8.3 %copy-start = (bf16[128,1024]{1,0:T(8,128)(2,1)S(1)}, bf16[128,1024]{1,0:T(8,128)(2,1)}, u32[]{:S(2)}) copy-start(bf16[128,1024]{1,0:T(8,128)(2,1)} %tok_ref.1) | copy-start | bytes 786436
  179.8 8.2 %copy-start.1 = (bf16[64,1024]{1,0:T(8,128)(2,1)S(1)}, bf16[64,1024]{1,0:T(8,128)(2,1)}, u32[]{:S(2)}) copy-start(bf16[64,1024]{1,0:T(8,128)(2,1)} %get-tuple-element.15.low_ref) | copy-start | bytes 393220
  179.8 75.8 %copy-start.4 = (f32[64,1024]{1,0:T(8,128)S(1)}, f32[64,1024]{1,0:T(8,128)}, u32[]{:S(2)}) copy-start(f32[64,1024]{1,0:T(8,128)} %get-tuple-element.23) | copy-start | bytes 786436

commit v3 on v2

--- a/solution.py
+++ b/solution.py
@@ -80,8 +80,8 @@
 
 
 def front_kernel(
-    p_ref, h_ref, w_ref, a, rows, cw, pruned_ref, low_ref,
-    hw, pack, chunk, got, mine, zgot, packed, piv,
+    p_ref, h_ref, w_ref, inv_out, rows_out, cw_out, pruned_ref, low_ref,
+    a, rows, cw, us, hw, pack, chunk, got, mine, zgot, packed, piv,
     ra, sb, rb, acc, rz, sz, rzn,
     rc, m0, ryu, ryd, sy, ry, acc_c, rcz,
     local, send1, recv1, send, recv,
@@ -159,8 +159,14 @@
 
     ga = [same(rows, chunk_at(0), 64, z_next), same(rows, chunk_at(0), 64, z_prev)]
     gb = [same(rows, chunk_at(3), 32, z_next), same(rows, chunk_at(1) + 32, 32, z_prev)]
-    gx = [same(rows, block_at(0), 256, x_up), same(rows, block_at(0), 256, x_down)]
-    gy = [same(rows, block_at(3), 128, x_up), same(rows, block_at(1) + 128, 128, x_down)]
+
+    def far_chunk(k, n):
+        return ((x + n) % 4) * 256 + ((zh + k) % 4) * 64
+
+    gx = [[same(rows, chunk_at(k), 64, x_up), same(rows, chunk_at(k), 64, x_down)] for k in (0, 1, 3, 2)]
+    gy = [
+        [same(rows, far_chunk(k, 3), 32, x_up), same(rows, far_chunk(k, 1) + 32, 32, x_down)] for k in (0, 1, 3, 2)
+    ]
 
     def held(r):
         return jnp.where(own_row, hw[at(r, 8), :], 0.0)
@@ -201,7 +207,7 @@
         zb_down.wait_recv()
         mid = zh * 64
         fill(rows, chunk_at(0), 64, lambda r: acc[at(mid + r, 8), :] + (rzn[0, at(r, 8), :] + rzn[1, at(r, 8), :]))
-        for copy in ga:
+        for copy in ga + gx[0]:
             copy.start()
 
     def handed(waits, starts):
@@ -264,32 +270,32 @@
     def piece(k):
         return at((k % 4) * 8, 8)
 
-    firsts = [copies(chunk.at[piece(x + d)], got.at[d - 1], xs[d - 1]) for d in (1, 2, 3)]
-    part = jnp.where(own_row, chunk[piece(x), :], 0.0)
+    firsts = [copies(chunk.at[piece(zh + d)], got.at[d - 1], zs[d - 1]) for d in (1, 2, 3)]
+    part = jnp.where(own_row, chunk[piece(zh), :], 0.0)
     for d in (1, 2, 3):
         firsts[d - 1].wait_recv()
-        part = part + jnp.where(row_of(zh, x - d + 4) == p, got[d - 1], 0.0)
+        part = part + jnp.where(row_of(zh - d + 4, x) == p, got[d - 1], 0.0)
     mine[...] = part
-    seconds = [copies(mine, zgot.at[d - 1], zs[d - 1]) for d in (1, 2, 3)]
+    seconds = [copies(mine, zgot.at[d - 1], xs[d - 1]) for d in (1, 2, 3)]
     for d in (1, 2, 3):
         seconds[d - 1].wait_recv()
         part = part + zgot[d - 1]
-    packed[j, piece(x), :] = part
-    thirds = [copies(packed.at[j, piece(x)], packed.at[j, piece(x)], xs[d - 1]) for d in (1, 2, 3)]
+    packed[j, piece(zh), :] = part
+    thirds = [copies(packed.at[j, piece(zh)], packed.at[j, piece(zh)], zs[d - 1]) for d in (1, 2, 3)]
+    rows_near()
     for copy in thirds:
         copy.wait_recv()
-    rows_near()
-    gather_cols(copies, packed, packed, PR)
+    gather_cols(copies, packed, packed, PR, rows_z_far)
 
     stages = [
-        (rows_z_far, cols_far),
-        (rows_z_near, cols_near),
+        (rows_z_near, cols_far),
+        (cols_near,),
         (rows_final, cols_across),
-        (lambda: handed(ga, gb), cols_final),
-        (lambda: handed(gb, gx), lambda: handed(cy, cy2 + [cc[3], cc[1]])),
-        (lambda: handed(cy2, [cc[2]]),),
-        (lambda: handed(gx, gy),),
-        (lambda: handed(cc, []),),
+        (lambda: handed(gx[0], gy[0]), cols_final),
+        (lambda: handed(ga, gb + gx[1] + gx[2]), lambda: handed(cy, cy2 + [cc[3], cc[1]])),
+        (lambda: handed(gb, gx[3]), lambda: handed(cy2, [cc[2]])),
+        (lambda: handed(gx[1] + gx[2], gy[1] + gy[2]),),
+        (lambda: handed(gx[3], gy[3]),),
     ]
 
     for g in range(4):
@@ -302,21 +308,36 @@
                     a[pl.ds(128 * q, 128), pl.ds(128 * r, 128)] = tile.T
     eye = (lax.broadcasted_iota(jnp.int32, (NB, NB), 0) == lax.broadcasted_iota(jnp.int32, (NB, NB), 1)).astype(f32)
 
+    put(piv, pivot_inverse([a[8 * w : 8 * w + 8, 0:NB] for w in range(NB // 8)]))
+
     def step(kb, _):
-        for n, stage in enumerate(stages):
+        for n, stage in enumerate(stages[:-1]):
 
             @pl.when(kb == n)
             def _():
                 for part in stage:
                     part()
 
-        sweep(a, piv, eye, kb)
+        sweep(a, piv, us, eye, kb, False)
         return 0
 
-    lax.fori_loop(0, PW // NB, step, 0)
-    handed(gy, [])
-
+    lax.fori_loop(0, PW // NB - 1, step, 0)
+    for part in stages[-1]:
+        part()
+    sweep(a, piv, us, eye, PW // NB - 1, True)
+    outs = [
+        pltpu.make_async_copy(cw, cw_out, local.at[0]),
+        pltpu.make_async_copy(a, inv_out, local.at[1]),
+        pltpu.make_async_copy(rows, rows_out, local.at[2]),
+    ]
+    handed(cc, [])
+    outs[0].start()
+    outs[1].start()
     lead = dot3(cw[pl.ds(PW, 64), :], a[...])
+    for pair in gy:
+        handed(pair, [])
+    outs[2].start()
+
     for t in range(4):
         lanes = pl.ds(256 * t, 256)
         value = hw[pl.ds(PW, 64), lanes] - dot3(lead, rows[:, lanes])
@@ -324,6 +345,8 @@
         low_ref[:, lanes] = value.astype(bf16)
 
     copies.drain()
+    for copy in outs:
+        copy.wait()
 
     @pl.when(i == j)
     def _():
@@ -331,29 +354,38 @@
             copy.wait_send()
 
 
-def sweep(a, piv, eye, kb):
+def put(piv, inv):
+    for w in range(NB // 8):
+        piv[8 * w : 8 * w + 8, :] = inv[w]
+
+
+def sweep(a, piv, us, eye, kb, last):
     n = PW
     here = pl.ds(pl.multiple_of(kb * NB, NB), NB)
-    blk = [a[pl.ds(pl.multiple_of(kb * NB + 8 * w, 8), 8), here] for w in range(NB // 8)]
-    inv = pivot_inverse(blk)
-    for w in range(NB // 8):
-        piv[8 * w : 8 * w + 8, :] = inv[w]
     a[here, here] = eye
     u = dot3(piv[...], a[here, :])
     uh, ul = split(u)
+    if not last:
+        us[...] = u
+        after = pl.ds(pl.multiple_of(kb * NB + NB, NB), NB)
+        block = a[after, after] - dot3(a[after, here], us[:, after])
     a[here, here] = -eye
     ch, cl = split(a[:, here])
     a[here, :] = jnp.zeros((NB, n), f32)
     a[:, here] = jnp.zeros((n, NB), f32)
     uk = jnp.concatenate([uh, ul, uh], axis=0)
     ck = jnp.concatenate([ch, ch, cl], axis=1)
+    if not last:
+        inv = pivot_inverse([block[8 * w : 8 * w + 8, :] for w in range(NB // 8)])
     for t in range(n // 256):
         r = slice(256 * t, 256 * t + 256)
         a[r, :] = a[r, :] - dot(ck[r, :], uk)
+    if not last:
+        put(piv, inv)
 
 
 def front(panels, inverse, weight):
-    sems = 9 + 25 + 16 + 14
+    sems = 9 + 25 + 28 + 14
     dma = pltpu.SemaphoreType.DMA
 
     def buf(*shape):
@@ -366,9 +398,9 @@
         front_kernel,
         out_shape=(out(PW, PW), out(PW, PW), out(8 * CB, PW), out(64, PW), jax.ShapeDtypeStruct((64, PW), bf16)),
         in_specs=[pl.BlockSpec(memory_space=pltpu.SMEM)] + [pl.BlockSpec(memory_space=pl.ANY)] * 2,
-        out_specs=(VMEM,) * 5,
+        out_specs=(pl.BlockSpec(memory_space=pl.ANY),) * 3 + (VMEM,) * 2,
         scratch_shapes=[
-            buf(8 * CB),
+            buf(PW), buf(PW), buf(8 * CB), buf(NB), buf(8 * CB),
             pltpu.VMEM((16 * PR, PC), f32),
             pltpu.VMEM((PR, PC), f32),
             pltpu.VMEM((3, 8, PC), f32),
@@ -386,7 +418,7 @@
     )(panels, inverse, weight)
 
 
-def gather_cols(copies, first, out, rows):
+def gather_cols(copies, first, out, rows, between):
     i, j, zh, x, y, zl, c = place()
     h = rows // 2
     ups, downs, cores = [], [], []
@@ -411,6 +443,7 @@
         s = col_of(y + 1, zl + t, c)
         halves.append(copies(out.at[s, pl.ds(h, h)], out.at[s, pl.ds(h, h)], down))
         cores.append(copies(out.at[s], out.at[s], peer))
+    between()
     for t in (0, 1):
         halves[2 * t].wait_recv()
         halves[2 * t + 1].wait_recv()
@@ -436,34 +469,51 @@
 
 
 def pivot_inverse(rows):
-    lane = lax.broadcasted_iota(jnp.int32, (8, NB), 1)
-    sub = lax.broadcasted_iota(jnp.int32, (8, NB), 0)
-    lane1 = lax.broadcasted_iota(jnp.int32, (1, NB), 1)
+    full = (8, NB)
+    lane = lax.broadcasted_iota(jnp.int32, full, 1)
+    sub = lax.broadcasted_iota(jnp.int32, full, 0)
     rows = list(rows)
+
+    def spread(k):
+        return [[jnp.broadcast_to(r[:, q : q + 1], full) for r in rows] for q in (k, k + 1)]
+
+    c0, c1 = spread(0)
     for k in range(0, NB, 2):
         v, s = k // 8, k % 8
-        c0 = [jnp.broadcast_to(r[:, k : k + 1], (8, NB)) for r in rows]
-        c1 = [jnp.broadcast_to(r[:, k + 1 : k + 2], (8, NB)) for r in rows]
-        r0, r1 = rows[v][s : s + 1, :], rows[v][s + 1 : s + 2, :]
-        p00, p01 = c0[v][s : s + 1, :], c1[v][s : s + 1, :]
-        p10, p11 = c0[v][s + 1 : s + 2, :], c1[v][s + 1 : s + 2, :]
+
+        def row(x, t):
+            return jnp.broadcast_to(x[s + t : s + t + 1, :], full)
+
+        r0, r1 = row(rows[v], 0), row(rows[v], 1)
+        p00, p01, p10, p11 = row(c0[v], 0), row(c1[v], 0), row(c0[v], 1), row(c1[v], 1)
         scale = 1.0 / (p00 * p11 - p01 * p10)
-        e0, e1 = lane1 == k, lane1 == k + 1
+        h00, h01, h10, h11 = p11 * scale, -(p01 * scale), -(p10 * scale), p00 * scale
+        ahead = spread(k + 2) if k + 2 < NB else ()
+        e0, e1 = lane == k, lane == k + 1
         r0 = jnp.where(e0, 1.0, jnp.where(e1, 0.0, r0))
         r1 = jnp.where(e1, 1.0, jnp.where(e0, 0.0, r1))
-        u0 = jnp.broadcast_to((p11 * scale) * r0 - (p01 * scale) * r1, (8, NB))
-        u1 = jnp.broadcast_to((p00 * scale) * r1 - (p10 * scale) * r0, (8, NB))
-        cols = (lane == k) | (lane == k + 1)
+        u0 = h00 * r0 + h01 * r1
+        u1 = h10 * r0 + h11 * r1
+        new = []
+        for d in ahead:
+            b0, b1 = row(d[v], 0), row(d[v], 1)
+            g0, g1 = h00 * b0 + h01 * b1, h10 * b0 + h11 * b1
+            n = [d[w] - c0[w] * g0 - c1[w] * g1 for w in range(NB // 8)]
+            n[v] = jnp.where(sub == s, g0, jnp.where(sub == s + 1, g1, n[v]))
+            new.append(n)
         for w in range(NB // 8):
-            base = jnp.where(cols, 0.0, rows[w]) - c0[w] * u0 - c1[w] * u1
+            base = jnp.where(e0 | e1, 0.0, rows[w]) - c0[w] * u0 - c1[w] * u1
             if w == v:
                 base = jnp.where(sub == s, u0, jnp.where(sub == s + 1, u1, base))
             rows[w] = base
+        if new:
+            c0, c1 = new
     return rows
 
 
 def refresh_kernel(
-    scale, low_ref, tok_ref, tgt_ref, res_ref, cor_ref, every, part, heard, own_low, lows,
+    scale, low_ref, tok_ref, tgt_ref, inv_ref, rows_ref, cw_ref, res_ref, cor_ref, prod_ref,
+    wide_a, wide_b, row_hi, row_lo, sol_hi, sol_lo, local, every, part, heard, own_low, lows,
     s_far, r_far_up, r_far_down, s_up, s_down, r_up, r_down, own,
     z_far, zr_far_up, zr_far_down, z_up, z_down, zr_up, zr_down,
     send, recv, rs_send, rs_recv, ag_send, ag_recv,
@@ -471,11 +521,39 @@
     i, j, zh, x, y, zl, c = place()
     x_up, x_down = (row_of(zh, x + 1), j), (row_of(zh, x + 3), j)
     z_next, z_prev = (row_of(zh + 1, x), j), (row_of(zh + 3, x), j)
+    fetch = [
+        pltpu.make_async_copy(rows_ref, wide_a, local.at[0]),
+        pltpu.make_async_copy(inv_ref, wide_b, local.at[1]),
+        pltpu.make_async_copy(cw_ref.at[pl.ds(0, PW)], wide_a, local.at[2]),
+    ]
+    fetch[0].start()
+    fetch[1].start()
     meet([(i, (j + d) % 16) for d in range(1, 16)] + [x_up, x_down, z_next, z_prev])
     copies = Copies(send, recv)
     tokens = tok_ref[...]
     half = low_ref.shape[0] // 2
     top, bottom = pl.ds(0, half), pl.ds(half, half)
+
+    def rows_split():
+        fetch[0].wait()
+        for t in range(4):
+            r = pl.ds(256 * t, 256)
+            row_hi[r, :], row_lo[r, :] = split(wide_a[r, :])
+        fetch[2].start()
+        fetch[1].wait()
+
+    def solve(t):
+        r = pl.ds(256 * t, 256)
+        bh, bl = split(wide_b[r, :])
+        value = dot(bh, row_hi[...]) + (dot(bh, row_lo[...]) + dot(bl, row_hi[...]))
+        sol_hi[r, :], sol_lo[r, :] = split(value)
+
+    def remove(t):
+        if t == 0:
+            fetch[2].wait()
+        r = pl.ds(256 * t, 256)
+        ch, cl = split(wide_a[r, :])
+        prod_ref[r, :] = dot(ch, sol_hi[...]) + (dot(ch, sol_lo[...]) + dot(cl, sol_hi[...]))
 
     partials = []
 
@@ -500,6 +578,8 @@
     zp = copies(low_ref, every.at[i], z_prev)
     sent = [spread(i, low_ref)]
     use(i, low_ref)
+    rows_split()
+    solve(0)
     zn.wait_recv()
     s = row_of(zh + 3, x)
     z1 = copies(every.at[s, top], every.at[s, top], z_next)
@@ -510,12 +590,14 @@
     sent.append(spread(s, every.at[s]))
     use(row_of(zh + 3, x), every.at[row_of(zh + 3, x)])
     use(s, every.at[s])
+    solve(1)
     z1.wait_recv()
     z2.wait_recv()
     s = row_of(zh + 2, x)
     sent.append(spread(s, every.at[s]))
     use(s, every.at[s])
     lasts = []
+    solve(2)
     for dz, (_, up, down) in zip((0, 3, 1, 2), sent):
         up.wait_recv()
         s = row_of(zh + dz, x + 3)
@@ -526,11 +608,14 @@
         b = copies(every.at[s, bottom], every.at[s, bottom], x_down)
         use(s, every.at[s])
         lasts.append((dz, a, b))
+    solve(3)
     for dz, a, b in lasts:
         a.wait_recv()
         b.wait_recv()
         s = row_of(zh + dz, x + 2)
         use(s, every.at[s])
+
+    remove(0)
 
     total = part[j] - tgt_ref[...]
     for d in range(1, 16):
@@ -560,6 +645,7 @@
         copy.start()
         shared.append(copy)
     lows[j] = total.astype(bf16)
+    remove(1)
     for d in range(1, 16):
         k = (j + d) % 16
         pltpu.make_async_remote_copy(
@@ -582,6 +668,7 @@
             copies(s_far.at[q, top], r_far_up.at[q], x_up),
             copies(s_far.at[q, bottom], r_far_down.at[q], x_down),
         ))
+    remove(2)
     near = []
     for q, dz in enumerate(order):
         value = product(zh + dz, x + 1)
@@ -596,6 +683,8 @@
         b = copies(s_down.at[q], r_down.at[q], x_down)
         near.append((a, b))
         own[q] = product(zh + dz, x)
+
+    remove(3)
 
     def joined(q):
         near[q][0].wait_recv()
@@ -627,7 +716,7 @@
         copy.wait_send()
 
 
-def refresh(low, tokens, targets_t, scale):
+def refresh(low, tokens, targets_t, block_inverse, rows, columns, scale):
     m, n = low.shape
     t = tokens.shape[0]
     sems = 4 + 16 + 16 + 4
@@ -638,10 +727,11 @@
 
     return pl.pallas_call(
         functools.partial(refresh_kernel, scale),
-        out_shape=(jax.ShapeDtypeStruct((m, t), f32), jax.ShapeDtypeStruct((m, n), f32)),
-        in_specs=[VMEM] * 3,
-        out_specs=(VMEM, VMEM),
+        out_shape=tuple(jax.ShapeDtypeStruct(shape, f32) for shape in ((m, t), (m, n), (n, n))),
+        in_specs=[VMEM] * 3 + [pl.BlockSpec(memory_space=pl.ANY)] * 3,
+        out_specs=(VMEM,) * 3,
         scratch_shapes=[
+            pltpu.VMEM((n, n), f32), pltpu.VMEM((n, n), f32), wide(n), wide(n), wide(n), wide(n), dma((3,)),
             wide(16, m), pltpu.VMEM((16, m, t), f32), pltpu.VMEM((16, m, t), f32),
             pltpu.VMEM((m, t), bf16), pltpu.VMEM((16, m, t), bf16),
             wide(4, m), wide(4, m // 2), wide(4, m // 2), wide(4, m), wide(4, m), wide(4, m), wide(4, m),
@@ -649,20 +739,19 @@
             wide(m), wide(m // 2), wide(m // 2), wide(m), wide(m), wide(m), wide(m),
             dma((sems,)), dma((sems,)), dma((16,)), dma((16,)), dma((15,)), dma((16,)),
         ],
-        compiler_params=pltpu.CompilerParams(collective_id=1, has_side_effects=True, vmem_limit_bytes=32 << 20),
+        compiler_params=pltpu.CompilerParams(collective_id=1, has_side_effects=True, vmem_limit_bytes=52 << 20),
         cost_estimate=pl.CostEstimate(flops=10**9, bytes_accessed=200 * 10**6, transcendentals=0),
         name="refresh",
-    )(low, tokens, targets_t)
+    )(low, tokens, targets_t, block_inverse, rows, columns)
 
 
 def shards(panels, inverse, weight, tokens, targets):
-    high = lax.Precision.HIGH
     block_inverse, row_panel, columns, pruned, low = front(panels, inverse, weight)
     token_count = tokens.shape[0] * lax.axis_size("row")
-    residual_t, correlation = refresh(low, tokens, targets.T.astype(f32), 1.0 / math.sqrt(token_count))
-    solved = jnp.dot(block_inverse, row_panel, precision=high, preferred_element_type=f32)
-    new_inverse = inverse - jnp.dot(columns[:PW], solved, precision=high, preferred_element_type=f32)
-    return (new_inverse, pruned, residual_t.T, correlation)
+    residual_t, correlation, update = refresh(
+        low, tokens, targets.T.astype(f32), block_inverse, row_panel, columns, 1.0 / math.sqrt(token_count)
+    )
+    return (inverse - update, pruned, residual_t.T, correlation)
 
 
 def solution(mesh):

time: 258 us -> 228 us (0.88)
  Pallas kernels: 235 us -> 215 us
  matrix products: 18.9 us -> 0 us
  other arithmetic: 0.01 us -> 6.33 us
    dot_general x2 -> x0, matrix products: 18.9 us -> none  [the longest x1 10.7 us: shards(): jnp.dot(block_inverse, row_panel, precision=high, preferred_element_type=...]
    pallas_call x1, Pallas kernels: 168 us -> 152 us  [front(): pl.pallas_call(front_kernel, out_shape=(out(PW, PW), out(PW, PW), out(8 *...]
    sub x0 -> x1, other arithmetic: none -> 5.61 us  [shards(): return (inverse - update, pruned, residual_t.T, correlation)]
    pallas_call x1, Pallas kernels: 67.5 us -> 63.2 us  [refresh(): pl.pallas_call(functools.partial(refresh_kernel, scale), out_shape=tuple(...]
where the time goes in v3:
time: 228 us; the launch traced here: 226 us
  Pallas kernels  215 us (94%)
  other arithmetic  6.33 us (3%)
  local copies, waits for them, and re-layouts  2.93 us (1%)
    pallas_call x1, Pallas kernels, front(): pl.pallas_call(front_kernel, out_shape=(out(PW, PW), out(PW, PW), out(8 *...  152 us
    pallas_call x1, Pallas kernels, refresh(): pl.pallas_call(functools.partial(refresh_kernel, scale), out_shape=tuple(...  63.2 us
    sub x1, other arithmetic, shards(): return (inverse - update, pruned, residual_t.T, correlation)  5.61 us

profile of v3, /device:TPU:8, one launch (start us, length us, event | category | flops | bytes accessed | tf_op | source)
XLA Modules:
  0.0 225.7 jit_solution(14703351690221825025)
XLA Ops:
  1.3 0.7 convert_bitcast_fusion.tgt_ref
  2.0 0.0 copy-start
  2.0 151.9 %front.1 = (f32[1024,1024]{1,0:T(8,128)}, f32[1024,1024]{1,0:T(8,128)}, f32[1088,1024]{1,0:T(8,128)}, f32[64,1024]{1,0:T(8,128)}, bf16[64,1024]{1,0:T(8,128)(2,1)}) custom-call(s32[1]{0:T(128)S(6)} %copy.12.p_ref, f32[1024,1024]{1,0:T(8,128)} %h_ref.1, f32[64,1024]{1,0:T(8,128)} %w_ref.1), custom_call_target="tpu_custom_call" | custom-call | flops 60000002048 | bytes 400000000 | tf_op jit(solution)/shard_map/front/pallas_call | solution.py:397
  153.9 0.0 copy-done
  153.9 0.0 copy-start.1
  153.9 0.9 copy-done.1
  154.8 0.0 copy-start.2
  154.8 63.2 %refresh.1 = (f32[64,128]{1,0:T(8,128)S(1)}, f32[64,1024]{1,0:T(8,128)S(1)}, f32[1024,1024]{1,0:T(8,128)}) custom-call(bf16[64,1024]{1,0:T(8,128)(2,1)S(1)} %copy-done.1, bf16[128,1024]{1,0:T(8,128)(2,1)S(1)} %copy-done, f32[64,128]{1,0:T(8,128)S(1)} %convert_bitcast_fusion.tgt_ref, f32[1024,1024]{1,0:T(8,128)} %get-tuple-element.13.inv_ref, ...), custom_call_target="tpu_custom_call" | custom-call | flops 1000000000 | bytes 200000000 | tf_op jit(solution)/shard_map/refresh/pallas_call | solution.py:728
  218.0 0.0 copy-done.2
  218.0 0.0 copy-start.3
  218.0 5.6 %sub.3 = f32[1024,1024]{1,0:T(8,128)} subtract(f32[1024,1024]{1,0:T(8,128)S(1)} %copy-done.2, f32[1024,1024]{1,0:T(8,128)} %get-tuple-element.16) | non-fusion elementwise | flops 1048576 | bytes 12582912 | tf_op jit(solution)/shard_map/sub | solution.py:754
  223.6 0.0 copy-done.3
  223.7 0.7 copy.13
  224.4 0.6 copy.14
  225.0 0.7 copy.15
Async XLA Ops:
  2.0 151.9 %copy-start = (bf16[128,1024]{1,0:T(8,128)(2,1)S(1)}, bf16[128,1024]{1,0:T(8,128)(2,1)}, u32[]{:S(2)}) copy-start(bf16[128,1024]{1,0:T(8,128)(2,1)} %tok_ref.1) | copy-start | bytes 786436
  153.9 0.9 copy-start.1
  154.8 63.2 %copy-start.2 = (f32[1024,1024]{1,0:T(8,128)S(1)}, f32[1024,1024]{1,0:T(8,128)}, u32[]{:S(2)}) copy-start(f32[1024,1024]{1,0:T(8,128)} %h_ref.1) | copy-start | bytes 12582916
  218.0 5.6 %copy-start.3 = (f32[64,1024]{1,0:T(8,128)S(1)}, f32[64,1024]{1,0:T(8,128)}, u32[]{:S(2)}) copy-start(f32[64,1024]{1,0:T(8,128)} %get-tuple-element.25) | copy-start | bytes 786436

commit v4 on v3

--- a/solution.py
+++ b/solution.py
@@ -140,8 +140,9 @@
     far = ((x + 2) % 4) * 256
     ra_up = copies(hw.at[at(far, 128)], ra.at[0], x_up)
     ra_down = copies(hw.at[at(far + 128, 128)], ra.at[1], x_down)
-    rb_up = copies.plan(sb.at[0], rb.at[0], x_up)
-    rb_down = copies.plan(sb.at[1], rb.at[1], x_down)
+    low_half, high_half = pl.ds(0, 128), pl.ds(128, 128)
+    rb_up = [copies.plan(sb.at[0, part], rb.at[0, part], x_up) for part in (high_half, low_half)]
+    rb_down = [copies.plan(sb.at[1, part], rb.at[1, part], x_down) for part in (low_half, high_half)]
     far = ((zh + 2) % 4) * 64
     za_up = copies.plan(acc.at[at(far, 32)], rz.at[0], z_next)
     za_down = copies.plan(acc.at[at(far + 32, 32)], rz.at[1], z_prev)
@@ -171,22 +172,24 @@
     def held(r):
         return jnp.where(own_row, hw[at(r, 8), :], 0.0)
 
+    up, down = block_at(1), block_at(3)
+    fill(sb.at[0], 128, 128, lambda r: held(up + 128 + r))
+    rb_up[0].start()
+    fill(sb.at[1], 0, 128, lambda r: held(down + r))
+    rb_down[0].start()
+
     def rows_near():
-        ra_up.wait_recv()
-        ra_down.wait_recv()
         before = row_of(zh, x + 3) == p
         after = row_of(zh, x + 1) == p
-        up, down = block_at(1), block_at(3)
+        ra_up.wait_recv()
         fill(sb.at[0], 0, 128, lambda r: held(up + r) + jnp.where(before, ra[0, at(r, 8), :], 0.0))
-        fill(sb.at[0], 128, 128, lambda r: held(up + 128 + r))
-        rb_up.start()
-        fill(sb.at[1], 0, 128, lambda r: held(down + r))
+        rb_up[1].start()
+        ra_down.wait_recv()
         fill(sb.at[1], 128, 128, lambda r: held(down + 128 + r) + jnp.where(after, ra[1, at(r, 8), :], 0.0))
-        rb_down.start()
+        rb_down[1].start()
 
     def rows_z_far():
-        rb_up.wait_recv()
-        rb_down.wait_recv()
+        handed(rb_up + rb_down, [])
         fill(acc, 0, 256, lambda r: held(block_at(0) + r) + (rb[0, at(r, 8), :] + rb[1, at(r, 8), :]))
         za_up.start()
         za_down.start()
@@ -271,31 +274,34 @@
         return at((k % 4) * 8, 8)
 
     firsts = [copies(chunk.at[piece(zh + d)], got.at[d - 1], zs[d - 1]) for d in (1, 2, 3)]
+    cols_far()
     part = jnp.where(own_row, chunk[piece(zh), :], 0.0)
     for d in (1, 2, 3):
         firsts[d - 1].wait_recv()
         part = part + jnp.where(row_of(zh - d + 4, x) == p, got[d - 1], 0.0)
     mine[...] = part
     seconds = [copies(mine, zgot.at[d - 1], xs[d - 1]) for d in (1, 2, 3)]
+    rows_near()
     for d in (1, 2, 3):
         seconds[d - 1].wait_recv()
         part = part + zgot[d - 1]
     packed[j, piece(zh), :] = part
     thirds = [copies(packed.at[j, piece(zh)], packed.at[j, piece(zh)], zs[d - 1]) for d in (1, 2, 3)]
-    rows_near()
+    cols_near()
     for copy in thirds:
         copy.wait_recv()
-    gather_cols(copies, packed, packed, PR, rows_z_far)
+    gather_cols(copies, packed, packed, PR, cols_across, rows_z_far)
+    rows_z_near()
 
     stages = [
-        (rows_z_near, cols_far),
-        (cols_near,),
-        (rows_final, cols_across),
-        (lambda: handed(gx[0], gy[0]), cols_final),
-        (lambda: handed(ga, gb + gx[1] + gx[2]), lambda: handed(cy, cy2 + [cc[3], cc[1]])),
+        (cols_final,),
+        (rows_final,),
+        (lambda: handed(cy, cy2 + [cc[3], cc[1]]),),
+        (lambda: handed(ga, gb + gx[1] + gx[2]), lambda: handed(gx[0], gy[0])),
         (lambda: handed(gb, gx[3]), lambda: handed(cy2, [cc[2]])),
         (lambda: handed(gx[1] + gx[2], gy[1] + gy[2]),),
         (lambda: handed(gx[3], gy[3]),),
+        (),
     ]
 
     for g in range(4):
@@ -385,7 +391,7 @@
 
 
 def front(panels, inverse, weight):
-    sems = 9 + 25 + 28 + 14
+    sems = 9 + 25 + 30 + 14
     dma = pltpu.SemaphoreType.DMA
 
     def buf(*shape):
@@ -418,7 +424,7 @@
     )(panels, inverse, weight)
 
 
-def gather_cols(copies, first, out, rows, between):
+def gather_cols(copies, first, out, rows, early, between):
     i, j, zh, x, y, zl, c = place()
     h = rows // 2
     ups, downs, cores = [], [], []
@@ -428,6 +434,7 @@
     for t in (0, 1):
         src = first if t == 0 else out
         if t == 1:
+            early()
             across.wait_recv()
         s = col_of(y, zl + t, c)
         ups.append(copies(src.at[s], out.at[s], up))

time: 228 us -> 219 us (0.961)
  Pallas kernels: 215 us -> 207 us
    pallas_call x1, Pallas kernels: 152 us -> 135 us  [front(): pl.pallas_call(front_kernel, out_shape=(out(PW, PW), out(PW, PW), out(8 *...]
    pallas_call x1, Pallas kernels: 63.2 us -> 72.1 us  [refresh(): pl.pallas_call(functools.partial(refresh_kernel, scale), out_shape=tuple(...]
where the time goes in v4:
time: 219 us; the launch traced here: 218 us
  Pallas kernels  207 us (95%)
  other arithmetic  6.33 us (3%)
  local copies, waits for them, and re-layouts  2.93 us (1%)
    pallas_call x1, Pallas kernels, front(): pl.pallas_call(front_kernel, out_shape=(out(PW, PW), out(PW, PW), out(8 *...  135 us
    pallas_call x1, Pallas kernels, refresh(): pl.pallas_call(functools.partial(refresh_kernel, scale), out_shape=tuple(...  72.1 us
    sub x1, other arithmetic, shards(): return (inverse - update, pruned, residual_t.T, correlation)  5.61 us

profile of v4, /device:TPU:8, one launch (start us, length us, event | category | flops | bytes accessed | tf_op | source)
XLA Modules:
  0.0 217.7 jit_solution(4333733169144403508)
XLA Ops:
  1.3 0.7 convert_bitcast_fusion.tgt_ref
  2.0 0.0 copy-start
  2.0 135.0 %front.1 = (f32[1024,1024]{1,0:T(8,128)}, f32[1024,1024]{1,0:T(8,128)}, f32[1088,1024]{1,0:T(8,128)}, f32[64,1024]{1,0:T(8,128)}, bf16[64,1024]{1,0:T(8,128)(2,1)}) custom-call(s32[1]{0:T(128)S(6)} %copy.12.p_ref, f32[1024,1024]{1,0:T(8,128)} %h_ref.1, f32[64,1024]{1,0:T(8,128)} %w_ref.1), custom_call_target="tpu_custom_call" | custom-call | flops 60000002048 | bytes 400000000 | tf_op jit(solution)/shard_map/front/pallas_call | solution.py:403
  137.0 0.0 copy-done
  137.1 0.0 copy-start.1
  137.1 0.9 copy-done.1
  138.0 0.0 copy-start.2
  138.0 72.1 %refresh.1 = (f32[64,128]{1,0:T(8,128)S(1)}, f32[64,1024]{1,0:T(8,128)S(1)}, f32[1024,1024]{1,0:T(8,128)}) custom-call(bf16[64,1024]{1,0:T(8,128)(2,1)S(1)} %copy-done.1, bf16[128,1024]{1,0:T(8,128)(2,1)S(1)} %copy-done, f32[64,128]{1,0:T(8,128)S(1)} %convert_bitcast_fusion.tgt_ref, f32[1024,1024]{1,0:T(8,128)} %get-tuple-element.13.inv_ref, ...), custom_call_target="tpu_custom_call" | custom-call | flops 1000000000 | bytes 200000000 | tf_op jit(solution)/shard_map/refresh/pallas_call | solution.py:735
  210.1 0.0 copy-done.2
  210.1 0.0 copy-start.3
  210.1 5.6 %sub.3 = f32[1024,1024]{1,0:T(8,128)} subtract(f32[1024,1024]{1,0:T(8,128)S(1)} %copy-done.2, f32[1024,1024]{1,0:T(8,128)} %get-tuple-element.16) | non-fusion elementwise | flops 1048576 | bytes 12582912 | tf_op jit(solution)/shard_map/sub | solution.py:761
  215.7 0.0 copy-done.3
  215.7 0.7 copy.13
  216.4 0.6 copy.14
  217.0 0.7 copy.15
Async XLA Ops:
  2.0 135.1 %copy-start = (bf16[128,1024]{1,0:T(8,128)(2,1)S(1)}, bf16[128,1024]{1,0:T(8,128)(2,1)}, u32[]{:S(2)}) copy-start(bf16[128,1024]{1,0:T(8,128)(2,1)} %tok_ref.1) | copy-start | bytes 786436
  137.1 0.9 copy-start.1
  138.0 72.1 %copy-start.2 = (f32[1024,1024]{1,0:T(8,128)S(1)}, f32[1024,1024]{1,0:T(8,128)}, u32[]{:S(2)}) copy-start(f32[1024,1024]{1,0:T(8,128)} %h_ref.1) | copy-start | bytes 12582916
  210.1 5.6 %copy-start.3 = (f32[64,1024]{1,0:T(8,128)S(1)}, f32[64,1024]{1,0:T(8,128)}, u32[]{:S(2)}) copy-start(f32[64,1024]{1,0:T(8,128)} %get-tuple-element.25) | copy-start | bytes 786436

commit v5 on v4

--- a/solution.py
+++ b/solution.py
@@ -73,10 +73,14 @@
 
 
 def fill(dst, start, rows, value):
-    @pl.loop(0, rows // 8)
+    if rows <= CB:
+        dst[at(start, rows), :] = value(0, rows)
+        return
+
+    @pl.loop(0, rows // 32)
     def _(t):
-        r = pl.multiple_of(t * 8, 8)
-        dst[at(start + r, 8), :] = value(r)
+        r = pl.multiple_of(t * 32, 32)
+        dst[at(start + r, 32), :] = value(r, 32)
 
 
 def front_kernel(
@@ -169,28 +173,28 @@
         [same(rows, far_chunk(k, 3), 32, x_up), same(rows, far_chunk(k, 1) + 32, 32, x_down)] for k in (0, 1, 3, 2)
     ]
 
-    def held(r):
-        return jnp.where(own_row, hw[at(r, 8), :], 0.0)
+    def held(r, n):
+        return jnp.where(own_row, hw[at(r, n), :], 0.0)
 
     up, down = block_at(1), block_at(3)
-    fill(sb.at[0], 128, 128, lambda r: held(up + 128 + r))
+    fill(sb.at[0], 128, 128, lambda r, n: held(up + 128 + r, n))
     rb_up[0].start()
-    fill(sb.at[1], 0, 128, lambda r: held(down + r))
+    fill(sb.at[1], 0, 128, lambda r, n: held(down + r, n))
     rb_down[0].start()
 
     def rows_near():
         before = row_of(zh, x + 3) == p
         after = row_of(zh, x + 1) == p
         ra_up.wait_recv()
-        fill(sb.at[0], 0, 128, lambda r: held(up + r) + jnp.where(before, ra[0, at(r, 8), :], 0.0))
+        fill(sb.at[0], 0, 128, lambda r, n: held(up + r, n) + jnp.where(before, ra[0, at(r, n), :], 0.0))
         rb_up[1].start()
         ra_down.wait_recv()
-        fill(sb.at[1], 128, 128, lambda r: held(down + 128 + r) + jnp.where(after, ra[1, at(r, 8), :], 0.0))
+        fill(sb.at[1], 128, 128, lambda r, n: held(down + 128 + r, n) + jnp.where(after, ra[1, at(r, n), :], 0.0))
         rb_down[1].start()
 
     def rows_z_far():
         handed(rb_up + rb_down, [])
-        fill(acc, 0, 256, lambda r: held(block_at(0) + r) + (rb[0, at(r, 8), :] + rb[1, at(r, 8), :]))
+        fill(acc, 0, 256, lambda r, n: held(block_at(0) + r, n) + (rb[0, at(r, n), :] + rb[1, at(r, n), :]))
         za_up.start()
         za_down.start()
 
@@ -198,18 +202,18 @@
         za_up.wait_recv()
         za_down.wait_recv()
         up, down = ((zh + 1) % 4) * 64, ((zh + 3) % 4) * 64
-        fill(sz.at[0], 0, 32, lambda r: acc[at(up + r, 8), :] + rz[0, at(r, 8), :])
-        fill(sz.at[0], 32, 32, lambda r: acc[at(up + 32 + r, 8), :])
+        fill(sz.at[0], 0, 32, lambda r, n: acc[at(up + r, n), :] + rz[0, at(r, n), :])
+        fill(sz.at[0], 32, 32, lambda r, n: acc[at(up + 32 + r, n), :])
         zb_up.start()
-        fill(sz.at[1], 0, 32, lambda r: acc[at(down + r, 8), :])
-        fill(sz.at[1], 32, 32, lambda r: acc[at(down + 32 + r, 8), :] + rz[1, at(r, 8), :])
+        fill(sz.at[1], 0, 32, lambda r, n: acc[at(down + r, n), :])
+        fill(sz.at[1], 32, 32, lambda r, n: acc[at(down + 32 + r, n), :] + rz[1, at(r, n), :])
         zb_down.start()
 
     def rows_final():
         zb_up.wait_recv()
         zb_down.wait_recv()
         mid = zh * 64
-        fill(rows, chunk_at(0), 64, lambda r: acc[at(mid + r, 8), :] + (rzn[0, at(r, 8), :] + rzn[1, at(r, 8), :]))
+        fill(rows, chunk_at(0), 64, lambda r, n: acc[at(mid + r, n), :] + (rzn[0, at(r, n), :] + rzn[1, at(r, n), :]))
         for copy in ga + gx[0]:
             copy.start()
 
@@ -238,7 +242,7 @@
         ca.wait_recv()
         own, other = j == p, col_of(y, zl, c + 1) == p
         base = c * 4 * CB
-        fill(m0, 0, 4 * CB, lambda r: jnp.where(own, hw[at(base + r, 8), :], 0.0) + jnp.where(other, rc[at(r, 8), :], 0.0))
+        fill(m0, 0, 4 * CB, lambda r, n: jnp.where(own, hw[at(base + r, n), :], 0.0) + jnp.where(other, rc[at(r, n), :], 0.0))
         ya_up.start()
         ya_down.start()
 
@@ -246,23 +250,23 @@
         ya_up.wait_recv()
         ya_down.wait_recv()
         up, down = ((y + 1) % 4) * CB, ((y + 3) % 4) * CB
-        fill(sy.at[0], 0, CT, lambda r: m0[at(up + r, 8), :] + ryu[at(r, 8), :])
-        fill(sy.at[0], CT, CB - CT, lambda r: m0[at(up + CT + r, 8), :])
+        fill(sy.at[0], 0, CT, lambda r, n: m0[at(up + r, n), :] + ryu[at(r, n), :])
+        fill(sy.at[0], CT, CB - CT, lambda r, n: m0[at(up + CT + r, n), :])
         yb_up.start()
-        fill(sy.at[1], 0, CT, lambda r: m0[at(down + r, 8), :])
-        fill(sy.at[1], CT, CB - CT, lambda r: m0[at(down + CT + r, 8), :] + ryd[at(r, 8), :])
+        fill(sy.at[1], 0, CT, lambda r, n: m0[at(down + r, n), :])
+        fill(sy.at[1], CT, CB - CT, lambda r, n: m0[at(down + CT + r, n), :] + ryd[at(r, n), :])
         yb_down.start()
 
     def cols_across():
         yb_up.wait_recv()
         yb_down.wait_recv()
         mid = y * CB
-        fill(acc_c, 0, CB, lambda r: m0[at(mid + r, 8), :] + (ry[0, at(r, 8), :] + ry[1, at(r, 8), :]))
+        fill(acc_c, 0, CB, lambda r, n: m0[at(mid + r, n), :] + (ry[0, at(r, n), :] + ry[1, at(r, n), :]))
         cz.start()
 
     def cols_final():
         cz.wait_recv()
-        fill(cw, col_at(0), CB, lambda r: acc_c[at(r, 8), :] + rcz[at(r, 8), :])
+        fill(cw, col_at(0), CB, lambda r, n: acc_c[at(r, n), :] + rcz[at(r, n), :])
         for copy in cy + cc[:1]:
             copy.start()
 
@@ -339,14 +343,14 @@
     handed(cc, [])
     outs[0].start()
     outs[1].start()
-    lead = dot3(cw[pl.ds(PW, 64), :], a[...])
+    lead = dot3_few(cw[pl.ds(PW, 64), :], a[...])
     for pair in gy:
         handed(pair, [])
     outs[2].start()
 
     for t in range(4):
         lanes = pl.ds(256 * t, 256)
-        value = hw[pl.ds(PW, 64), lanes] - dot3(lead, rows[:, lanes])
+        value = hw[pl.ds(PW, 64), lanes] - dot3_few(lead, rows[:, lanes])
         pruned_ref[:, lanes] = value
         low_ref[:, lanes] = value.astype(bf16)
 
@@ -475,6 +479,14 @@
     return dot(ah, bh) + (dot(ah, bl) + dot(al, bh))
 
 
+def dot3_few(a, b):
+    m = a.shape[0]
+    ah, al = split(a)
+    bh, bl = split(b)
+    both = dot(jnp.concatenate([ah, al], axis=0), bh)
+    return both[:m] + (dot(ah, bl) + both[m:])
+
+
 def pivot_inverse(rows):
     full = (8, NB)
     lane = lax.broadcasted_iota(jnp.int32, full, 1)
@@ -585,37 +597,34 @@
     zp = copies(low_ref, every.at[i], z_prev)
     sent = [spread(i, low_ref)]
     use(i, low_ref)
+    zn.wait_recv()
+    before = row_of(zh + 3, x)
+    z1 = copies(every.at[before, top], every.at[before, top], z_next)
+    sent.append(spread(before, every.at[before]))
+    zp.wait_recv()
+    after = row_of(zh + 1, x)
+    z2 = copies(every.at[after, bottom], every.at[after, bottom], z_prev)
+    sent.append(spread(after, every.at[after]))
+    use(before, every.at[before])
+    use(after, every.at[after])
     rows_split()
-    solve(0)
-    zn.wait_recv()
-    s = row_of(zh + 3, x)
-    z1 = copies(every.at[s, top], every.at[s, top], z_next)
-    sent.append(spread(s, every.at[s]))
-    zp.wait_recv()
-    s = row_of(zh + 1, x)
-    z2 = copies(every.at[s, bottom], every.at[s, bottom], z_prev)
-    sent.append(spread(s, every.at[s]))
-    use(row_of(zh + 3, x), every.at[row_of(zh + 3, x)])
-    use(s, every.at[s])
-    solve(1)
     z1.wait_recv()
     z2.wait_recv()
     s = row_of(zh + 2, x)
     sent.append(spread(s, every.at[s]))
     use(s, every.at[s])
     lasts = []
-    solve(2)
-    for dz, (_, up, down) in zip((0, 3, 1, 2), sent):
+    for t, (dz, (_, up, down)) in enumerate(zip((0, 3, 1, 2), sent)):
         up.wait_recv()
-        s = row_of(zh + dz, x + 3)
-        a = copies(every.at[s, top], every.at[s, top], x_up)
-        use(s, every.at[s])
+        before = row_of(zh + dz, x + 3)
+        a = copies(every.at[before, top], every.at[before, top], x_up)
         down.wait_recv()
-        s = row_of(zh + dz, x + 1)
-        b = copies(every.at[s, bottom], every.at[s, bottom], x_down)
-        use(s, every.at[s])
+        after = row_of(zh + dz, x + 1)
+        b = copies(every.at[after, bottom], every.at[after, bottom], x_down)
+        use(before, every.at[before])
+        use(after, every.at[after])
         lasts.append((dz, a, b))
-    solve(3)
+        solve(t)
     for dz, a, b in lasts:
         a.wait_recv()
         b.wait_recv()

time: 219 us -> 218 us (level)
  no operation moved by 1% of the time
where the time goes in v5:
time: 218 us
  Pallas kernels  207 us (95%)
  other arithmetic  6.33 us (3%)
  local copies, waits for them, and re-layouts  2.93 us (1%)
    pallas_call x1, Pallas kernels, front(): pl.pallas_call(front_kernel, out_shape=(out(PW, PW), out(PW, PW), out(8 *...  137 us
    pallas_call x1, Pallas kernels, refresh(): pl.pallas_call(functools.partial(refresh_kernel, scale), out_shape=tuple(...  70.7 us
    sub x1, other arithmetic, shards(): return (inverse - update, pruned, residual_t.T, correlation)  5.61 us

profile of v5, /device:TPU:8, one launch (start us, length us, event | category | flops | bytes accessed | tf_op | source)
XLA Modules:
  0.0 218.0 jit_solution(15246694470386695679)
XLA Ops:
  1.3 0.7 convert_bitcast_fusion.tgt_ref
  2.0 0.0 copy-start
  2.0 136.8 %front.1 = (f32[1024,1024]{1,0:T(8,128)}, f32[1024,1024]{1,0:T(8,128)}, f32[1088,1024]{1,0:T(8,128)}, f32[64,1024]{1,0:T(8,128)}, bf16[64,1024]{1,0:T(8,128)(2,1)}) custom-call(s32[1]{0:T(128)S(6)} %copy.12.p_ref, f32[1024,1024]{1,0:T(8,128)} %h_ref.1, f32[64,1024]{1,0:T(8,128)} %w_ref.1), custom_call_target="tpu_custom_call" | custom-call | flops 60000002048 | bytes 400000000 | tf_op jit(solution)/shard_map/front/pallas_call | solution.py:407
  138.8 0.0 copy-done
  138.8 0.0 copy-start.1
  138.8 0.9 copy-done.1
  139.7 0.0 copy-start.2
  139.7 70.7 %refresh.1 = (f32[64,128]{1,0:T(8,128)S(1)}, f32[64,1024]{1,0:T(8,128)S(1)}, f32[1024,1024]{1,0:T(8,128)}) custom-call(bf16[64,1024]{1,0:T(8,128)(2,1)S(1)} %copy-done.1, bf16[128,1024]{1,0:T(8,128)(2,1)S(1)} %copy-done, f32[64,128]{1,0:T(8,128)S(1)} %convert_bitcast_fusion.tgt_ref, f32[1024,1024]{1,0:T(8,128)} %get-tuple-element.13.inv_ref, ...), custom_call_target="tpu_custom_call" | custom-call | flops 1000000000 | bytes 200000000 | tf_op jit(solution)/shard_map/refresh/pallas_call | solution.py:744
  210.4 0.0 copy-done.2
  210.4 0.0 copy-start.3
  210.4 5.6 %sub.3 = f32[1024,1024]{1,0:T(8,128)} subtract(f32[1024,1024]{1,0:T(8,128)S(1)} %copy-done.2, f32[1024,1024]{1,0:T(8,128)} %get-tuple-element.16) | non-fusion elementwise | flops 1048576 | bytes 12582912 | tf_op jit(solution)/shard_map/sub | solution.py:770
  216.0 0.0 copy-done.3
  216.0 0.7 copy.13
  216.7 0.6 copy.14
  217.3 0.7 copy.15
Async XLA Ops:
  2.0 136.8 %copy-start = (bf16[128,1024]{1,0:T(8,128)(2,1)S(1)}, bf16[128,1024]{1,0:T(8,128)(2,1)}, u32[]{:S(2)}) copy-start(bf16[128,1024]{1,0:T(8,128)(2,1)} %tok_ref.1) | copy-start | bytes 786436
  138.8 0.9 copy-start.1
  139.7 70.7 %copy-start.2 = (f32[1024,1024]{1,0:T(8,128)S(1)}, f32[1024,1024]{1,0:T(8,128)}, u32[]{:S(2)}) copy-start(f32[1024,1024]{1,0:T(8,128)} %h_ref.1) | copy-start | bytes 12582916
  210.4 5.6 %copy-start.3 = (f32[64,1024]{1,0:T(8,128)S(1)}, f32[64,1024]{1,0:T(8,128)}, u32[]{:S(2)}) copy-start(f32[64,1024]{1,0:T(8,128)} %get-tuple-element.25) | copy-start | bytes 786436

commit v6 on v5

--- a/solution.py
+++ b/solution.py
@@ -295,17 +295,16 @@
     for copy in thirds:
         copy.wait_recv()
     gather_cols(copies, packed, packed, PR, cols_across, rows_z_far)
-    rows_z_near()
 
     stages = [
-        (cols_final,),
-        (rows_final,),
-        (lambda: handed(cy, cy2 + [cc[3], cc[1]]),),
-        (lambda: handed(ga, gb + gx[1] + gx[2]), lambda: handed(gx[0], gy[0])),
-        (lambda: handed(gb, gx[3]), lambda: handed(cy2, [cc[2]])),
+        (rows_z_near, cols_final),
+        (),
+        (rows_final, lambda: handed(cy, cy2 + [cc[3], cc[1]])),
+        (lambda: handed(gx[0], gy[0]),),
+        (lambda: handed(ga, gb + gx[1] + gx[2]), lambda: handed(cy2, [cc[2]])),
+        (lambda: handed(gb, gx[3]),),
         (lambda: handed(gx[1] + gx[2], gy[1] + gy[2]),),
         (lambda: handed(gx[3], gy[3]),),
-        (),
     ]
 
     for g in range(4):

time: 218 us -> 204 us (0.936)
  Pallas kernels: 207 us -> 192 us
    pallas_call x1, Pallas kernels: 137 us -> 128 us  [front(): pl.pallas_call(front_kernel, out_shape=(out(PW, PW), out(PW, PW), out(8 *...]
    pallas_call x1, Pallas kernels: 70.7 us -> 64 us  [refresh(): pl.pallas_call(functools.partial(refresh_kernel, scale), out_shape=tuple(...]
where the time goes in v6:
time: 204 us; the launch traced here: 203 us
  Pallas kernels  192 us (94%)
  other arithmetic  6.33 us (3%)
  local copies, waits for them, and re-layouts  2.93 us (1%)
    pallas_call x1, Pallas kernels, front(): pl.pallas_call(front_kernel, out_shape=(out(PW, PW), out(PW, PW), out(8 *...  128 us
    pallas_call x1, Pallas kernels, refresh(): pl.pallas_call(functools.partial(refresh_kernel, scale), out_shape=tuple(...  64 us
    sub x1, other arithmetic, shards(): return (inverse - update, pruned, residual_t.T, correlation)  5.61 us

profile of v6, /device:TPU:8, one launch (start us, length us, event | category | flops | bytes accessed | tf_op | source)
XLA Modules:
  0.0 202.6 jit_solution(14036088414049302232)
XLA Ops:
  1.3 0.7 convert_bitcast_fusion.tgt_ref
  2.0 0.0 copy-start
  2.0 128.0 %front.1 = (f32[1024,1024]{1,0:T(8,128)}, f32[1024,1024]{1,0:T(8,128)}, f32[1088,1024]{1,0:T(8,128)}, f32[64,1024]{1,0:T(8,128)}, bf16[64,1024]{1,0:T(8,128)(2,1)}) custom-call(s32[1]{0:T(128)S(6)} %copy.12.p_ref, f32[1024,1024]{1,0:T(8,128)} %h_ref.1, f32[64,1024]{1,0:T(8,128)} %w_ref.1), custom_call_target="tpu_custom_call" | custom-call | flops 60000002048 | bytes 400000000 | tf_op jit(solution)/shard_map/front/pallas_call | solution.py:406
  130.0 0.0 copy-done
  130.1 0.0 copy-start.1
  130.1 0.9 copy-done.1
  131.0 0.0 copy-start.2
  131.0 64.0 %refresh.1 = (f32[64,128]{1,0:T(8,128)S(1)}, f32[64,1024]{1,0:T(8,128)S(1)}, f32[1024,1024]{1,0:T(8,128)}) custom-call(bf16[64,1024]{1,0:T(8,128)(2,1)S(1)} %copy-done.1, bf16[128,1024]{1,0:T(8,128)(2,1)S(1)} %copy-done, f32[64,128]{1,0:T(8,128)S(1)} %convert_bitcast_fusion.tgt_ref, f32[1024,1024]{1,0:T(8,128)} %get-tuple-element.13.inv_ref, ...), custom_call_target="tpu_custom_call" | custom-call | flops 1000000000 | bytes 200000000 | tf_op jit(solution)/shard_map/refresh/pallas_call | solution.py:743
  195.0 0.0 copy-done.2
  195.0 0.0 copy-start.3
  195.0 5.6 %sub.3 = f32[1024,1024]{1,0:T(8,128)} subtract(f32[1024,1024]{1,0:T(8,128)S(1)} %copy-done.2, f32[1024,1024]{1,0:T(8,128)} %get-tuple-element.16) | non-fusion elementwise | flops 1048576 | bytes 12582912 | tf_op jit(solution)/shard_map/sub | solution.py:769
  200.6 0.0 copy-done.3
  200.6 0.7 copy.13
  201.3 0.6 copy.14
  201.9 0.7 copy.15
Async XLA Ops:
  2.0 128.1 %copy-start = (bf16[128,1024]{1,0:T(8,128)(2,1)S(1)}, bf16[128,1024]{1,0:T(8,128)(2,1)}, u32[]{:S(2)}) copy-start(bf16[128,1024]{1,0:T(8,128)(2,1)} %tok_ref.1) | copy-start | bytes 786436
  130.1 0.9 copy-start.1
  131.0 64.0 %copy-start.2 = (f32[1024,1024]{1,0:T(8,128)S(1)}, f32[1024,1024]{1,0:T(8,128)}, u32[]{:S(2)}) copy-start(f32[1024,1024]{1,0:T(8,128)} %h_ref.1) | copy-start | bytes 12582916
  195.0 5.6 %copy-start.3 = (f32[64,1024]{1,0:T(8,128)S(1)}, f32[64,1024]{1,0:T(8,128)}, u32[]{:S(2)}) copy-start(f32[64,1024]{1,0:T(8,128)} %get-tuple-element.25) | copy-start | bytes 786436
